TPU v7x, 32 devices: a whole 2x2x4 slice. The times are simulated.
32 devices in a mesh: tile: 16 (over z, x, core), probe: 2 (over y).
Axes of the slice: x: 2, y: 2, z: 4, core: 2. Of those that a mesh axis runs over, the one named last changes fastest.
Arguments:
- latent: float32 [16, 16, 4, 320], P(None, 'tile'), may hold values from -60 to 60, as said below
- probes: bfloat16 [2, 16, 16, 16, 4, 320], P(None, 'probe', None, 'tile'), may hold values from -60 to 60, as said below
- gn_gain: float32 [320], replicated, may hold values from 0.1 to 1.9
- gn_bias: float32 [320], replicated, may hold values from -3 to 3
- w_spatial: bfloat16 [9, 320, 320], replicated, may hold values from -0.109375 to 0.109375
- spatial_bias: float32 [320], replicated, may hold values from -3 to 3
- w_temporal: bfloat16 [3, 320, 320], replicated, may hold values from -0.1875 to 0.1875
- temporal_bias: float32 [320], replicated, may hold values from -3 to 3
- w_qkv: bfloat16 [320, 3, 320], replicated, may hold values from -0.3125 to 0.3125
- w_out: bfloat16 [320, 320], replicated, may hold values from -0.3125 to 0.3125
- temper: float32 [8], replicated, may hold values from 1 to 4
Outputs:
- block_out: bfloat16 [16, 16, 4, 320], P(None, 'tile')
- basis: float32 [16, 16, 16, 4, 320], P('probe', None, 'tile')
- basis_images: bfloat16 [16, 16, 16, 4, 320], P('probe', None, 'tile')
- test_images: bfloat16 [16, 16, 16, 4, 320], P('probe', None, 'tile')
- rayleigh: float32 [2, 16], replicated
- divergence: float32 [], replicated
Inputs may be any that keep to these rules, and one draw needn't show every extreme that they name: `latent`: every element is drawn within the bounds. `probes`: every element is drawn within the bounds.
All inputs are finite; a program needn't handle non-finite values.
Results may differ from a plain program's by a relative error of at most 0.012.
Values may be sent and summed in bfloat16 or wider, within the bound.
A program may use at most 128 MiB of HBM per device.

v0:
```python
import functools
import math

import jax
import jax.numpy as jnp
import numpy as np
from jax import lax
from jax.experimental import pallas as pl
from jax.experimental.pallas import tpu as pltpu
from jax.sharding import PartitionSpec as P

C = 320
GROUPS = 32
HEADS = 8
HEAD_DIM = 40
EPS = 1e-05
HIGHEST = lax.Precision.HIGHEST
F32 = jnp.float32
BF16 = jnp.bfloat16
CHUNK = HEADS


def dot(a, b):
    return jnp.dot(a, b, preferred_element_type=F32)


def hdot(a, b):
    return jnp.dot(a, b, preferred_element_type=F32, precision=HIGHEST)


def ndot(a, b, precision=None):
    return lax.dot_general(
        a, b, (((1,), (1,)), ((), ())), preferred_element_type=F32, precision=precision
    )


def iota(shape, dim):
    return lax.broadcasted_iota(jnp.int32, shape, dim)


def same_block(rows, columns, block):
    return (iota((rows, columns), 0) // block) == (iota((rows, columns), 1) // block)


def group_matrix():
    return (np.arange(C)[:, None] // (C // GROUPS) == np.arange(GROUPS)[None, :]).astype(np.float32)


def head_matrix():
    heads = np.arange(C) // HEAD_DIM
    return (heads[:, None] == heads[None, :]).astype(np.float32)


def head_rows():
    return (np.arange(HEADS)[:, None] == np.arange(C)[None, :] // HEAD_DIM).astype(np.float32)


def call(kernel, out_shape, *args, grid=None, in_specs=None, out_specs=None, flops=10**8):
    total = sum(a.size * a.dtype.itemsize for a in args)
    extra = {}
    if grid is not None:
        extra = dict(grid=grid, in_specs=in_specs, out_specs=out_specs)
    return pl.pallas_call(
        kernel,
        out_shape=out_shape,
        compiler_params=pltpu.CompilerParams(vmem_limit_bytes=56 * 2**20),
        cost_estimate=pl.CostEstimate(flops=flops, bytes_accessed=total, transcendentals=0),
        **extra,
    )(*args)


def sums_kernel(frames, with_latent, x_ref, t_ref, g_ref, out_ref):
    cols = x_ref.shape[0]
    count = t_ref.shape[1] // frames
    first = jnp.zeros((count, frames, C), F32)
    cross = jnp.zeros((count, frames, C), F32)
    lat = jnp.zeros((frames, C), F32)
    square = jnp.zeros((frames, C), F32)
    for w in range(cols):
        t = t_ref[w].astype(F32).reshape(count, frames, C)
        x = x_ref[w]
        first = first + t
        cross = cross + t * x[None]
        lat = lat + x
        square = square + x * x
    rows = [jnp.sum(first, axis=1), jnp.sum(cross, axis=1)]
    if with_latent:
        rows.append(jnp.broadcast_to(jnp.sum(lat, axis=0, keepdims=True), (8, C)))
        rows.append(jnp.broadcast_to(jnp.sum(square, axis=0, keepdims=True), (8, C)))
    out_ref[...] = hdot(jnp.concatenate(rows, axis=0), g_ref[...])


def latent_stats(ls_ref, members, gt):
    sums = ls_ref[...]
    mean = sums[0:1] / members
    inv = lax.rsqrt(sums[8:9] / members - mean * mean + EPS)
    return mean, inv


def conv_rows(act, w_ref, cols, per):
    total = None
    left = None
    right = None
    span = cols * per
    for a in range(3):
        mid = dot(act[a], w_ref[3 * a + 1])
        lo = dot(act[a][: span - per], w_ref[3 * a])
        hi = dot(act[a][per:], w_ref[3 * a + 2])
        total = mid if total is None else total + mid
        left = lo if left is None else left + lo
        right = hi if right is None else right + hi
    zero = jnp.zeros((per, C), F32)
    return (
        total + jnp.concatenate([zero, left], axis=0) + jnp.concatenate([right, zero], axis=0)
    )


def conv_frames(signal, w_ref, frames):
    rows = signal.shape[0]
    place = lax.rem(iota((rows, C), 0), frames)
    before = pltpu.roll(dot(signal, w_ref[0]), 1, 0)
    after = pltpu.roll(dot(signal, w_ref[2]), rows - 1, 0)
    return (
        dot(signal, w_ref[1])
        + jnp.where(place > 0, before, 0.0)
        + jnp.where(place < frames - 1, after, 0.0)
    )


def primal_kernel(
    members,
    edge_ref,
    temper_ref,
    lo_ref,
    x_ref,
    hi_ref,
    ls_ref,
    gain_ref,
    bias_ref,
    sb_ref,
    tb_ref,
    ws_ref,
    wt_ref,
    wqkv_ref,
    wo_ref,
    gt_ref,
    hh_ref,
    out_ref,
    a_ref,
    b_ref,
    qk_ref,
    kexp_ref,
    qexp_ref,
    vexp_ref,
    w_ref,
    wbd_ref,
):
    cols, frames = x_ref.shape[0], x_ref.shape[1]
    rows = cols * frames
    hf = HEADS * frames
    mean, inv = latent_stats(ls_ref, members, None)
    mean = hdot(mean + jnp.zeros((8, GROUPS), F32), gt_ref[...])[0:1]
    inv = hdot(inv + jnp.zeros((8, GROUPS), F32), gt_ref[...])[0:1]
    gain = gain_ref[...]
    acts = []
    for r, ref in enumerate((lo_ref, x_ref, hi_ref)):
        centered = ref[...].reshape(rows, C) - mean
        normed = centered * inv * gain + bias_ref[...]
        sig = jax.nn.sigmoid(normed)
        slope = sig * (1.0 + normed * (1.0 - sig)) * gain
        active = normed * sig
        if r != 1:
            keep = edge_ref[r // 2]
            slope = slope * keep
            active = active * keep
        a_ref[r] = (slope * inv).reshape(cols, frames, C)
        b_ref[r] = (slope * centered).reshape(cols, frames, C)
        acts.append(active.astype(BF16))
    spatial = (conv_rows(acts, ws_ref, cols, frames) + sb_ref[...]).astype(BF16)
    residual = x_ref[...].reshape(rows, C) + tb_ref[...] + conv_frames(spatial, wt_ref, frames)
    rounded = residual.astype(BF16)
    q = dot(rounded, wqkv_ref[0])
    k = dot(rounded, wqkv_ref[1])
    v = dot(rounded, wqkv_ref[2])
    hh = hh_ref[...]
    rq = 1.0 / jnp.sqrt(hdot(q * q, hh) / HEAD_DIM + 1.0)
    rk = 1.0 / jnp.sqrt(hdot(k * k, hh) / HEAD_DIM + 1.0)
    shape = (cols, frames, C)
    qk_ref[0] = q.reshape(shape)
    qk_ref[1] = (q * rq * rq * rq).reshape(shape)
    qk_ref[2] = rq.reshape(shape)
    qk_ref[3] = k.reshape(shape)
    qk_ref[4] = (k * rk * rk * rk).reshape(shape)
    qk_ref[5] = rk.reshape(shape)
    qu = q * rq
    ku = k * rk
    head_of_row = iota((hf, C), 0) // frames
    channel = iota((hf, C), 1)
    mask = jnp.where(
        (channel >= head_of_row * HEAD_DIM) & (channel < (head_of_row + 1) * HEAD_DIM), 1.0, 0.0
    )
    scale = jnp.zeros((hf, C), F32)
    for h in range(HEADS):
        scale = jnp.where(head_of_row == h, temper_ref[h] / math.sqrt(HEAD_DIM), scale)
    scale = scale * mask
    segment = jnp.where(same_block(hf, hf, frames), 1.0, 0.0)
    ei = iota((hf, HEADS * hf), 0)
    ej = iota((hf, HEADS * hf), 1)
    spread = jnp.where(
        (ei // frames == ej // hf) & (lax.rem(ei, frames) == lax.rem(ej, frames)), 1.0, 0.0
    ).astype(BF16)
    di = iota((hf, HEADS * hf), 0) // frames
    dj = lax.rem(ej, hf) // frames
    diagonal = jnp.where(di == dj, 1.0, 0.0)
    mixes = []
    for w in range(cols):
        part = slice(w * frames, (w + 1) * frames)
        k_rows = jnp.concatenate([ku[part]] * HEADS, axis=0) * scale
        q_rows = jnp.concatenate([qu[part]] * HEADS, axis=0) * scale
        v_rows = jnp.concatenate([v[part]] * HEADS, axis=0) * mask
        kexp_ref[w] = k_rows.astype(BF16)
        qexp_ref[w] = q_rows.astype(BF16)
        vexp_ref[w] = v_rows.astype(BF16)
        exponent = jnp.exp(ndot(qu[part], k_rows, HIGHEST))
        weights = exponent / hdot(exponent, segment)
        w_ref[w] = weights
        mixes.append(hdot(weights, v_rows))
        wide = dot(weights.astype(BF16), spread)
        wbd_ref[w] = (jnp.concatenate([wide] * CHUNK, axis=0) * diagonal).astype(BF16)
    mixture = jnp.concatenate(mixes, axis=0).astype(BF16)
    out_ref[...] = (residual + dot(mixture, wo_ref[...])).astype(BF16).reshape(shape)


def tangent_kernel(
    members,
    lo_ref,
    t_ref,
    hi_ref,
    first_ref,
    cross_ref,
    ls_ref,
    ws_ref,
    wt_ref,
    wqkv_ref,
    wo_ref,
    gt_ref,
    hh_ref,
    hrow_ref,
    a_ref,
    b_ref,
    qk_ref,
    kexp_ref,
    qexp_ref,
    vexp_ref,
    w_ref,
    wbd_ref,
    out_ref,
):
    cols, frames = a_ref.shape[1], a_ref.shape[2]
    per = CHUNK * frames
    hf = HEADS * frames
    mean, inv = latent_stats(ls_ref, members, None)
    first = first_ref[...]
    d_mean = first / members
    d_var = 2.0 * (cross_ref[...] - mean * first) / members
    d_std = -0.5 * inv * inv * inv * d_var
    d_mean = hdot(d_mean, gt_ref[...])[:, None, :]
    d_std = hdot(d_std, gt_ref[...])[:, None, :]
    acts = []
    for r, ref in enumerate((lo_ref, t_ref, hi_ref)):
        pieces = []
        for w in range(cols):
            t = ref[w].astype(F32).reshape(CHUNK, frames, C)
            piece = a_ref[r, w][None] * (t - d_mean) + b_ref[r, w][None] * d_std
            pieces.append(piece.reshape(per, C).astype(BF16))
        acts.append(jnp.concatenate(pieces, axis=0))
    spatial = conv_rows(acts, ws_ref, cols, per).astype(BF16)
    residual = t_ref[...].reshape(cols * per, C).astype(F32) + conv_frames(spatial, wt_ref, frames)
    rounded = residual.astype(BF16)
    shape = (cols, CHUNK, frames, C)
    hh = hh_ref[...].astype(BF16)

    def unit_shift(base, projection):
        value, cube, inverse = (qk_ref[base + i][:, None] for i in range(3))
        moved = dot(rounded, projection).reshape(shape)
        along = dot((value * moved).reshape(cols * per, C).astype(BF16), hh) * (1.0 / HEAD_DIM)
        return (moved * inverse - cube * along.reshape(shape)).reshape(cols * per, C).astype(BF16)

    dqu = unit_shift(0, wqkv_ref[0])
    dku = unit_shift(3, wqkv_ref[1])
    dv = dot(rounded, wqkv_ref[2])
    on_diagonal = same_block(hf, per, frames)
    segment = jnp.where(same_block(hf, hf, frames), 1.0, 0.0).astype(BF16)
    mixes = []
    for w in range(cols):
        part = slice(w * per, (w + 1) * per)
        scores = ndot(dqu[part], kexp_ref[w])
        turned = ndot(qexp_ref[w], dku[part])
        for d in range(HEADS):
            moved = pltpu.roll(turned, d * frames, 1) if d else turned
            moved = jnp.where(on_diagonal, moved, 0.0)
            if d:
                moved = jnp.concatenate([moved[d * frames :], moved[: d * frames]], axis=0)
            scores = scores + moved
        weights = jnp.concatenate([w_ref[w]] * CHUNK, axis=0)
        weighted = weights * scores
        top = weighted.astype(BF16)
        rest = (weighted - top.astype(F32)).astype(BF16)
        shift = weighted - weights * (dot(top, segment) + dot(rest, segment))
        own = dv[part]
        heads = [(own * hrow_ref[h : h + 1]).astype(BF16) for h in range(HEADS)]
        mix = dot(shift.astype(BF16), vexp_ref[w]) + dot(
            wbd_ref[w], jnp.concatenate(heads, axis=0)
        )
        mixes.append(mix.astype(BF16))
    result = residual + dot(jnp.concatenate(mixes, axis=0), wo_ref[...])
    out_ref[...] = result.reshape(cols, per, C).astype(out_ref.dtype)


def gather_rows(ref, w):
    return jnp.concatenate([ref[p, w] for p in range(ref.shape[0])], axis=0)


def gram_kernel(frames, s_ref, t_ref, out_ref):
    cols = t_ref.shape[0]
    total = None
    for w in range(cols):
        s = gather_rows(s_ref, w)
        term = ndot(jnp.concatenate([s, t_ref[w]], axis=0), s)
        total = term if total is None else total + term
    rows, columns = total.shape
    same = lax.rem(iota((rows, columns), 0), frames) == lax.rem(iota((rows, columns), 1), frames)
    total = jnp.where(same, total, 0.0)
    summed = jnp.sum(total.reshape(rows // frames, frames, columns), axis=1)
    fold = jnp.where(
        iota((columns, columns // frames), 0) // frames == iota((columns, columns // frames), 1),
        1.0,
        0.0,
    )
    out_ref[...] = hdot(summed, fold)


def combine_kernel(
    frames, total, slot_ref, gram_ref, s_ref, js_ref, t_ref, jt_ref, basis_ref, bi_ref, ti_ref, f_ref
):
    cols = t_ref.shape[0]
    ns = gram_ref.shape[1]
    own = gram_ref.shape[0] - ns
    gram = gram_ref[:ns, :]
    cross = gram_ref[ns:, :]
    inverse = jnp.where(iota((ns, ns), 0) == iota((ns, ns), 1), 1.0, 0.0)
    row = iota((ns, ns), 0)
    for j in range(ns):
        scale = 1.0 / jnp.sqrt(gram[j : j + 1, j : j + 1])
        column = gram[:, j : j + 1] * scale
        upper = gram[j : j + 1, :] * scale
        lower = inverse[j : j + 1, :] * scale
        gram = jnp.where(row > j, gram - column * upper, gram)
        inverse = jnp.where(row > j, inverse - column * lower, jnp.where(row == j, lower, inverse))
    first = slot_ref[0]
    pick = jnp.where(iota((own, ns), 1) == iota((own, ns), 0) + first, 1.0, 0.0)
    to_basis = math.sqrt(total) * hdot(pick, inverse)
    to_project = hdot(ndot(cross, inverse, HIGHEST), inverse)
    big, wide = own * frames, ns * frames
    spread_rows = jnp.where(iota((big, own), 0) // frames == iota((big, own), 1), 1.0, 0.0)
    spread_columns = jnp.where(iota((ns, wide), 1) // frames == iota((ns, wide), 0), 1.0, 0.0)
    same = lax.rem(iota((big, wide), 0), frames) == lax.rem(iota((big, wide), 1), frames)

    def expand(matrix):
        full = jnp.where(same, hdot(spread_rows, hdot(matrix, spread_columns)), 0.0)
        parts = []
        for _ in range(3):
            piece = full.astype(BF16)
            parts.append(piece)
            full = full - piece.astype(F32)
        return parts

    basis_parts = expand(to_basis)
    project_parts = expand(to_project)

    def apply(parts, array):
        result = dot(parts[0], array)
        for piece in parts[1:]:
            result = result + dot(piece, array)
        return result

    sums = [jnp.zeros((big, C), F32) for _ in range(3)]
    for w in range(cols):
        s = gather_rows(s_ref, w)
        js = gather_rows(js_ref, w)
        basis = apply(basis_parts, s)
        projected = t_ref[w].astype(F32) - apply(project_parts, s)
        basis_image = apply(basis_parts[:2], js)
        test_image = jt_ref[w] - apply(project_parts[:2], js)
        basis_ref[w] = basis
        bi_ref[w] = basis_image.astype(BF16)
        ti_ref[w] = test_image.astype(BF16)
        sums[0] = sums[0] + basis * basis_image
        sums[1] = sums[1] + projected * test_image
        sums[2] = sums[2] + projected * projected
    lane = iota((own, 128), 1)
    forms = jnp.zeros((own, 128), F32)
    for i in range(3):
        value = jnp.sum(jnp.sum(sums[i].reshape(own, frames, C), axis=1), axis=1, keepdims=True)
        forms = jnp.where(lane == i, value, forms)
    f_ref[...] = forms


def on_device(
    latent,
    probes,
    gn_gain,
    gn_bias,
    w_spatial,
    spatial_bias,
    w_temporal,
    temporal_bias,
    w_qkv,
    w_out,
    temper,
):
    frames, cols = latent.shape[0], latent.shape[2]
    own = probes.shape[1]
    tiles, shares = lax.axis_size("tile"), lax.axis_size("probe")
    ns = own * shares
    padded = -(-own // CHUNK) * CHUNK
    total = latent.size * tiles
    members = total // GROUPS
    hf = HEADS * frames
    here = lax.axis_index("tile")
    first_slot = lax.axis_index("probe") * own

    x = jnp.swapaxes(latent[:, 0], 0, 1)
    p = jnp.transpose(probes[:, :, :, 0], (3, 0, 1, 2, 4))
    if padded != own:
        p = jnp.pad(p, ((0, 0), (0, 0), (0, padded - own), (0, 0), (0, 0)))
    p = p.reshape(cols, 2 * padded * frames, C)
    forward = [(i, i + 1) for i in range(tiles - 1)]
    backward = [(j, i) for i, j in forward]

    def neighbours(block):
        return lax.ppermute(block, "tile", forward), lax.ppermute(block, "tile", backward)

    x_lo, x_hi = neighbours(x)
    p_lo, p_hi = neighbours(p)
    group = jnp.asarray(group_matrix())
    group_t = jnp.asarray(group_matrix().T)
    hh = jnp.asarray(head_matrix())
    hrow = jnp.asarray(head_rows())
    sums = call(
        functools.partial(sums_kernel, frames, True),
        jax.ShapeDtypeStruct((4 * padded + 16, GROUPS), F32),
        x,
        p,
        group,
    )
    sums = lax.psum(sums, "tile")
    latent_sums = sums[4 * padded :]
    wqkv = jnp.swapaxes(w_qkv, 0, 1)
    edge = jnp.stack([here > 0, here < tiles - 1]).astype(F32)

    smem = pl.BlockSpec(memory_space=pltpu.SMEM)
    vmem = pl.BlockSpec(memory_space=pltpu.VMEM)
    primal = pl.pallas_call(
        functools.partial(primal_kernel, members),
        in_specs=[smem, smem] + [vmem] * 14,
        out_shape=[
            jax.ShapeDtypeStruct((cols, frames, C), BF16),
            jax.ShapeDtypeStruct((3, cols, frames, C), F32),
            jax.ShapeDtypeStruct((3, cols, frames, C), F32),
            jax.ShapeDtypeStruct((6, cols, frames, C), F32),
            jax.ShapeDtypeStruct((cols, hf, C), BF16),
            jax.ShapeDtypeStruct((cols, hf, C), BF16),
            jax.ShapeDtypeStruct((cols, hf, C), BF16),
            jax.ShapeDtypeStruct((cols, frames, hf), F32),
            jax.ShapeDtypeStruct((cols, hf, HEADS * hf), BF16),
        ],
        compiler_params=pltpu.CompilerParams(vmem_limit_bytes=56 * 2**20),
        cost_estimate=pl.CostEstimate(flops=10**8, bytes_accessed=10**7, transcendentals=0),
    )(
        edge,
        temper,
        x_lo,
        x,
        x_hi,
        latent_sums,
        gn_gain[None],
        gn_bias[None],
        spatial_bias[None],
        temporal_bias[None],
        w_spatial,
        w_temporal,
        wqkv,
        w_out,
        group_t,
        hh,
    )
    block_out, caches = primal[0], primal[1:]
    chunks = padded // CHUNK
    per = CHUNK * frames

    def tangent(lo, mid, hi, offset, first, cross, dtype):
        fixed = (latent_sums, w_spatial, w_temporal, wqkv, w_out, group_t, hh, hrow) + tuple(caches)
        moving = pl.BlockSpec((cols, per, C), lambda i: (0, i + offset, 0))
        stat = pl.BlockSpec((CHUNK, GROUPS), lambda i: (i, 0))
        return call(
            functools.partial(tangent_kernel, members),
            jax.ShapeDtypeStruct((cols, padded * frames, C), dtype),
            lo,
            mid,
            hi,
            first,
            cross,
            *fixed,
            grid=(chunks,),
            in_specs=[moving] * 3 + [stat] * 2 + [vmem] * len(fixed),
            out_specs=pl.BlockSpec((cols, per, C), lambda i: (0, i, 0)),
            flops=2 * 10**9,
        )

    sketch = tangent(
        p_lo, p, p_hi, 0, sums[:padded], sums[2 * padded : 3 * padded], BF16
    )
    s_lo, s_hi = neighbours(sketch)
    s_sums = call(
        functools.partial(sums_kernel, frames, False),
        jax.ShapeDtypeStruct((2 * padded, GROUPS), F32),
        x,
        sketch,
        group,
    )
    s_sums = lax.psum(s_sums, "tile")
    s_all = lax.all_gather(sketch[:, : own * frames], "probe", axis=0)
    test = tangent(
        p_lo,
        p,
        p_hi,
        chunks,
        sums[padded : 2 * padded],
        sums[3 * padded : 4 * padded],
        F32,
    )
    p_test = p[:, padded * frames :]
    gram = call(
        functools.partial(gram_kernel, frames),
        jax.ShapeDtypeStruct((ns + padded, ns), F32),
        s_all,
        p_test,
    )
    gram = lax.psum(gram, "tile")
    second = tangent(s_lo, sketch, s_hi, 0, s_sums[:padded], s_sums[padded:], BF16)
    js_all = lax.all_gather(second[:, : own * frames], "probe", axis=0)
    image = (cols, padded * frames, C)
    basis, basis_images, test_images, forms = pl.pallas_call(
        functools.partial(combine_kernel, frames, total),
        in_specs=[smem] + [vmem] * 5,
        out_shape=[
            jax.ShapeDtypeStruct(image, F32),
            jax.ShapeDtypeStruct(image, BF16),
            jax.ShapeDtypeStruct(image, BF16),
            jax.ShapeDtypeStruct((padded, 128), F32),
        ],
        compiler_params=pltpu.CompilerParams(vmem_limit_bytes=56 * 2**20),
        cost_estimate=pl.CostEstimate(flops=10**9, bytes_accessed=10**7, transcendentals=0),
    )(first_slot.astype(jnp.int32)[None], gram, s_all, js_all, p_test, test)

    own_slots = first_slot + jnp.arange(own, dtype=jnp.int32)
    placed = jnp.arange(ns, dtype=jnp.int32)[None, :] == own_slots[:, None]
    placed = jnp.sum(jnp.where(placed[None], forms[:own, :3].T[:, :, None], 0.0), axis=1)
    placed = lax.psum(placed, ("tile", "probe"))
    rayleigh = jnp.stack([placed[0] / total, placed[1] / placed[2]])
    divergence = (jnp.sum(placed[0]) / total + jnp.sum(placed[1]) / ns) / total

    def restore(array):
        array = array.reshape(cols, padded, frames, C)[:, :own]
        return jnp.transpose(array, (1, 2, 0, 3))[:, :, None]

    return (
        jnp.swapaxes(block_out, 0, 1)[:, None],
        restore(basis),
        restore(basis_images),
        restore(test_images),
        rayleigh,
        divergence,
    )


def solution(mesh):
    in_specs = (
        P(None, "tile", None, None),
        P(None, "probe", None, "tile", None, None),
        P(),
        P(),
        P(),
        P(),
        P(),
        P(),
        P(),
        P(),
        P(),
    )
    out_specs = (
        P(None, "tile", None, None),
        P("probe", None, "tile", None, None),
        P("probe", None, "tile", None, None),
        P("probe", None, "tile", None, None),
        P(),
        P(),
    )
    return jax.shard_map(
        on_device, mesh=mesh, in_specs=in_specs, out_specs=out_specs, check_vma=False
    )
```

profile of v0, /device:TPU:0, one launch (start us, length us, event | category | flops | bytes accessed | tf_op | source)
XLA Modules:
  0.0 275.8 jit_solution(18021013733438906800)
XLA Ops:
  0.6 0.9 copy.67
  1.5 2.4 collective-permute-start
  3.9 1.3 collective-permute-start.1
  5.2 0.0 copy-start.7
  5.3 0.0 copy-start.8
  5.3 0.0 copy-start.9
  5.3 0.0 copy-start.10
  5.3 1.3 copy.46
  6.6 0.0 copy-start
  6.6 0.3 copy.47
  6.8 5.2 %collective-permute-start.2 = (bf16[4,256,320]{1,2,0:T(8,128)(2,1)S(1)}, bf16[4,256,320]{1,2,0:T(8,128)(2,1)S(1)}, u32[]{:S(2)}, u32[]{:S(2)}) collective-permute-start(bf16[4,256,320]{1,2,0:T(8,128)(2,1)S(1)} %copy.47), channel_id=1, source_target_pairs={{0,2},{2,4},{4,6},{6,8},{8,10},{10,12},{12,14},{14,16},{16,18},{18... | collective-permute-start | bytes 1966088 | tf_op jit(solution)/shard_map/ppermute | solution.py:442
  12.0 1.3 collective-permute-start.3
  13.3 0.8 slice.53.t_ref
  14.1 0.0 copy-done
  14.1 2.4 shard_map.190
  16.5 64.6 %psum.28 = f32[48,32]{1,0:T(8,128)S(1)} all-reduce(f32[48,32]{1,0:T(8,128)} %shard_map.190), channel_id=1, replica_groups=mesh['tile'=16,'probe'=2] {'tile'}, use_global_device_ids=true, to_apply=%region_0.0 | all-reduce | flops 1536 | bytes 12288 | tf_op jit(solution)/shard_map/psum | solution.py:457
  81.1 0.6 slice.50.ls_ref
  81.7 0.0 copy-done.7
  81.7 0.6 broadcast_in_dim.51.gain_ref
  82.3 0.6 broadcast_in_dim.52.bias_ref
  82.8 0.0 copy-done.9
  82.8 0.5 broadcast_in_dim.53.sb_ref
  83.4 0.6 broadcast_in_dim.54.tb_ref
  84.0 0.1 iota_compare_fusion
  84.0 0.6 fusion
  84.6 0.6 add_convert_fusion.edge_ref
  85.2 0.0 collective-permute-done.lo_ref
  85.2 0.0 collective-permute-done.1.hi_ref
  85.3 0.6 copy-done.4
  85.9 0.1 copy-done.5
  85.9 8.3 %shard_map.191 = (bf16[4,16,320]{2,1,0:T(8,128)(2,1)}, f32[3,4,16,320]{3,2,1,0:T(8,128)}, f32[3,4,16,320]{3,2,1,0:T(8,128)}, f32[6,4,16,320]{3,2,1,0:T(8,128)}, ...) custom-call(f32[2]{0:T(128)} %add_convert_fusion.edge_ref, ...), custom_call_target="tpu_custom_call" | custom-call | flops 100000000 | bytes 10000000 | tf_op jit(solution)/shard_map/pallas_call | solution.py:464
  94.3 1.4 copy.61
  95.7 0.0 collective-permute-done.2
  95.7 1.2 copy.49.lo_ref
  96.9 0.0 collective-permute-done.3
  96.9 1.2 copy.50.hi_ref
  98.1 11.5 %shard_map.192.t_ref = bf16[4,128,320]{2,1,0:T(8,128)(2,1)} custom-call(bf16[4,256,320]{2,1,0:T(8,128)(2,1)} %copy.49.lo_ref, bf16[4,256,320]{2,1,0:T(8,128)(2,1)} %bitcast.39, bf16[4,256,320]{2,1,0:T(8,128)(2,1)} %copy.50.hi_ref, f32[8,32]{1,0:T(8,128)} %get-tuple-element.57.first_ref, f32[8,32]{1,0:T(8,128)} %get-tuple-element.56.cross_ref, ...), custom_call_target="tpu_custom_call" | custom-call | flops 2000000000 | bytes 8755200 | tf_op jit(solution)/shard_map/pallas_call | solution.py:63
  109.5 1.2 copy.51
  110.8 2.0 shard_map.194
  112.8 1.4 collective-permute-start.4
  114.2 1.3 collective-permute-start.5
  115.5 11.1 %all-gather = bf16[8,128,320]{1,2,0:T(8,128)(2,1)S(1)} all-gather(bf16[4,128,320]{1,2,0:T(8,128)(2,1)S(1)} %copy.51), channel_id=2, replica_groups=mesh['tile'=16,'probe'=2] {'probe'}, dimensions={0}, use_global_device_ids=true | all-gather | bytes 983040 | tf_op jit(solution)/shard_map/all_gather | solution.py:533
  126.6 1.2 copy.52
  127.8 2.7 shard_map.193
  130.5 57.7 %all-reduce = (f32[24,16]{1,0:T(8,128)}, f32[16,32]{1,0:T(8,128)S(1)}) all-reduce(f32[24,16]{1,0:T(8,128)} %shard_map.193, f32[16,32]{1,0:T(8,128)S(1)} %copy-done.6), channel_id=1, replica_groups=mesh['tile'=16,'probe'=2] {'tile'}, use_global_device_ids=true, to_apply=%region_1.0 | all-reduce | flops 896 | bytes 7168 | tf_op jit(solution)/shard_map/psum | solution.py:550
  188.2 11.6 %shard_map.196.jt_ref = f32[4,128,320]{2,1,0:T(8,128)} custom-call(bf16[4,256,320]{2,1,0:T(8,128)(2,1)} %copy.49.lo_ref, bf16[4,256,320]{2,1,0:T(8,128)(2,1)} %bitcast.40, bf16[4,256,320]{2,1,0:T(8,128)(2,1)} %copy.50.hi_ref, f32[8,32]{1,0:T(8,128)} %get-tuple-element.55.first_ref, f32[8,32]{1,0:T(8,128)} %get-tuple-element.54.cross_ref, ...), custom_call_target="tpu_custom_call" | custom-call | flops 2000000000 | bytes 8755200 | tf_op jit(solution)/shard_map/pallas_call | solution.py:63
  199.8 0.6 fusion.1
  200.4 0.0 collective-permute-done.4.lo_ref
  200.4 0.0 collective-permute-done.5.hi_ref
  200.4 0.7 copy-done.2
  201.1 0.1 copy-done.3
  201.3 11.7 %shard_map.195 = bf16[4,128,320]{2,1,0:T(8,128)(2,1)} custom-call(bf16[4,128,320]{2,1,0:T(8,128)(2,1)} %copy-done.2, bf16[4,128,320]{2,1,0:T(8,128)(2,1)} %shard_map.192.t_ref, bf16[4,128,320]{2,1,0:T(8,128)(2,1)} %copy-done.3, f32[8,32]{1,0:T(8,128)} %get-tuple-element.59.first_ref, f32[8,32]{1,0:T(8,128)} %get-tuple-element.58.cross_ref, ...), custom_call_target="tpu_custom_call" | custom-call | flops 2000000000 | bytes 7772160 | tf_op jit(solution)/shard_map/pallas_call | solution.py:63
  213.0 1.2 copy.53
  214.2 7.7 %all-gather.1 = bf16[8,128,320]{1,2,0:T(8,128)(2,1)S(1)} all-gather(bf16[4,128,320]{1,2,0:T(8,128)(2,1)S(1)} %copy.53), channel_id=3, replica_groups=mesh['tile'=16,'probe'=2] {'probe'}, dimensions={0}, use_global_device_ids=true | all-gather | bytes 983040 | tf_op jit(solution)/shard_map/all_gather | solution.py:552
  221.9 1.2 copy.54
  223.1 6.3 %shard_map.197 = (f32[4,128,320]{2,1,0:T(8,128)}, bf16[4,128,320]{2,1,0:T(8,128)(2,1)}, bf16[4,128,320]{2,1,0:T(8,128)(2,1)}, f32[8,128]{1,0:T(8,128)}) custom-call(s32[1]{0:T(128)} %bitcast.11.slot_ref, f32[24,16]{1,0:T(8,128)} %get-tuple-element.52.gram_ref, bf16[2,4,128,320]{3,2,1,0:T(8,128)(2,1)} %bitcast.46, bf16[2,4,128,320]{3,2,1,0:T(8,128)(2,1)} %bitcast.55, ...), custom_call_target="tpu_custom_call" | custom-call | flops 1000000000 | bytes 10000000 | tf_op jit(solution)/shard_map/pallas_call | solution.py:554
  229.3 0.7 slice_bitcast_fusion
  230.0 0.1 copy.60
  230.1 0.1 select_reduce_fusion
  230.2 36.8 %psum.31 = f32[3,16]{1,0:T(4,128)S(1)} all-reduce(f32[3,16]{1,0:T(4,128)S(1)} %select_reduce_fusion), channel_id=1, replica_groups=mesh['tile'=16,'probe'=2] {'tile','probe'}, use_global_device_ids=true, to_apply=%region_4.5 | all-reduce | flops 48 | bytes 384 | tf_op jit(solution)/shard_map/psum | solution.py:570
  267.0 0.6 slice_reduce_fusion
  268.9 2.5 copy.66
  271.5 0.6 pad_maximum_fusion
  272.0 2.6 copy_bitcast_fusion.1
  (11 shorter events, 0.0 us)
Async XLA Ops:
  1.5 12.6 %copy-start.1 = (f32[16,1,4,320]{3,0,2,1:T(8,128)}, f32[16,1,4,320]{3,0,2,1:T(8,128)S(1)}, u32[]{:S(2)}) copy-start(f32[16,1,4,320]{3,0,2,1:T(8,128)S(1)} %copy.67) | copy-start | bytes 245764
  1.5 83.7 %collective-permute-start = (f32[4,16,320]{2,1,0:T(8,128)S(1)}, f32[4,16,320]{2,1,0:T(8,128)S(1)}, u32[]{:S(2)}, u32[]{:S(2)}) collective-permute-start(f32[4,16,320]{2,1,0:T(8,128)S(1)} %bitcast.47), channel_id=1, source_target_pairs={{0,2},{2,4},{4,6},{6,8},{8,10},{10,12},{12,14},{14,16},{16,18},{18... | collective-permute-start | bytes 245768 | tf_op jit(solution)/shard_map/ppermute | solution.py:442
  3.9 81.3 %collective-permute-start.1 = (f32[4,16,320]{2,1,0:T(8,128)S(1)}, f32[4,16,320]{2,1,0:T(8,128)S(1)}, u32[]{:S(2)}, u32[]{:S(2)}) collective-permute-start(f32[4,16,320]{2,1,0:T(8,128)S(1)} %bitcast.48), channel_id=1, source_target_pairs={{2,0},{4,2},{6,4},{8,6},{10,8},{12,10},{14,12},{16,14},{18,16},{20... | collective-permute-start | bytes 245768 | tf_op jit(solution)/shard_map/ppermute | solution.py:442
  5.2 76.4 %copy-start.7 = (f32[320]{0:T(512)S(1)}, f32[320]{0:T(512)}, u32[]{:S(2)}) copy-start(f32[320]{0:T(512)} %param.17) | copy-start | bytes 3844
  5.3 77.0 %copy-start.8 = (f32[320]{0:T(512)S(1)}, f32[320]{0:T(512)}, u32[]{:S(2)}) copy-start(f32[320]{0:T(512)} %param.18) | copy-start | bytes 3844
  5.3 77.5 %copy-start.9 = (f32[320]{0:T(512)S(1)}, f32[320]{0:T(512)}, u32[]{:S(2)}) copy-start(f32[320]{0:T(512)} %param.20) | copy-start | bytes 3844
  5.3 78.1 %copy-start.10 = (f32[320]{0:T(512)S(1)}, f32[320]{0:T(512)}, u32[]{:S(2)}) copy-start(f32[320]{0:T(512)} %param.22) | copy-start | bytes 3844
  6.6 7.6 %copy-start = (bf16[4,2,8,16,320]{4,3,2,1,0:T(8,128)(2,1)}, bf16[4,2,8,16,320]{4,3,2,1,0:T(8,128)(2,1)S(1)}, u32[]{:S(2)}) copy-start(bf16[4,2,8,16,320]{4,3,2,1,0:T(8,128)(2,1)S(1)} %copy.46) | copy-start | bytes 1966084
  6.8 88.9 %collective-permute-start.2 = (bf16[4,256,320]{1,2,0:T(8,128)(2,1)S(1)}, bf16[4,256,320]{1,2,0:T(8,128)(2,1)S(1)}, u32[]{:S(2)}, u32[]{:S(2)}) collective-permute-start(bf16[4,256,320]{1,2,0:T(8,128)(2,1)S(1)} %copy.47), channel_id=1, source_target_pairs={{0,2},{2,4},{4,6},{6,8},{8,10},{10,12},{12,14},{14,16},{16,18},{18... | collective-permute-start | bytes 1966088 | tf_op jit(solution)/shard_map/ppermute | solution.py:442
  12.0 84.9 %collective-permute-start.3 = (bf16[4,256,320]{1,2,0:T(8,128)(2,1)S(1)}, bf16[4,256,320]{1,2,0:T(8,128)(2,1)S(1)}, u32[]{:S(2)}, u32[]{:S(2)}) collective-permute-start(bf16[4,256,320]{1,2,0:T(8,128)(2,1)S(1)} %copy.47), channel_id=1, source_target_pairs={{2,0},{4,2},{6,4},{8,6},{10,8},{12,10},{14,12},{16,14},{18,16},{20... | collective-permute-start | bytes 1966088 | tf_op jit(solution)/shard_map/ppermute | solution.py:442
  85.2 0.6 copy-start.4
  85.2 0.7 copy-start.5
  112.8 17.7 %copy-start.6 = (f32[16,32]{1,0:T(8,128)S(1)}, f32[16,32]{1,0:T(8,128)}, u32[]{:S(2)}) copy-start(f32[16,32]{1,0:T(8,128)} %shard_map.194) | copy-start | bytes 6148
  112.8 87.6 %collective-permute-start.4 = (bf16[4,128,320]{2,1,0:T(8,128)(2,1)}, bf16[4,128,320]{2,1,0:T(8,128)(2,1)S(1)}, u32[]{:S(2)}, u32[]{:S(2)}) collective-permute-start(bf16[4,128,320]{2,1,0:T(8,128)(2,1)} %shard_map.192.t_ref), channel_id=1, source_target_pairs={{0,2},{2,4},{4,6},{6,8},{8,10},{10,12},{12,14},{14,16},{16,18},{18... | collective-permute-start | bytes 983048 | tf_op jit(solution)/shard_map/ppermute | solution.py:442
  114.2 86.2 %collective-permute-start.5 = (bf16[4,128,320]{2,1,0:T(8,128)(2,1)}, bf16[4,128,320]{2,1,0:T(8,128)(2,1)S(1)}, u32[]{:S(2)}, u32[]{:S(2)}) collective-permute-start(bf16[4,128,320]{2,1,0:T(8,128)(2,1)} %shard_map.192.t_ref), channel_id=1, source_target_pairs={{2,0},{4,2},{6,4},{8,6},{10,8},{12,10},{14,12},{16,14},{18,16},{20... | collective-permute-start | bytes 983048 | tf_op jit(solution)/shard_map/ppermute | solution.py:442
  200.4 0.7 copy-start.2
  200.4 0.9 copy-start.3
where the time goes:
time: 277 us; the launch traced here: 276 us
  blocking collectives  178 us (64%)
  Pallas kernels  56.5 us (20%)
  local copies, waits for them, and re-layouts  23.3 us (8%)
  starting transfers between devices  12.9 us (5%)
  between operations  3.23 us (1%)
    psum x1, blocking collectives, on_device(): sums = lax.psum(sums, 'tile')  64.6 us
    psum x1, blocking collectives, on_device(): gram = lax.psum(gram, 'tile')  57.7 us
    pallas_call x6, Pallas kernels, call(): pl.pallas_call(kernel, out_shape=out_shape, compiler_params=pltpu.Compile...  41.9 us
    psum x1, blocking collectives, on_device(): placed = lax.psum(placed, ('tile', 'probe'))  36.8 us
    all_gather x1, blocking collectives, on_device(): s_all = lax.all_gather(sketch[:, :own * frames], 'probe', axis=0)  11.1 us
    ppermute x3, starting transfers between devices, neighbours(): lax.ppermute(block, 'tile', forward)  9 us
    pallas_call x1, Pallas kernels, on_device(): pl.pallas_call(functools.partial(primal_kernel, members), in_specs=[smem,...  8.34 us
    all_gather x1, blocking collectives, on_device(): js_all = lax.all_gather(second[:, :own * frames], 'probe', axis=0)  7.74 us
  transfers between devices with their start and end apart: 6, of which 0 were waited for; matrix products, arithmetic and copies ran while one was open for 4% of the time, Pallas kernels for 9%

commit v1 on v0

--- a/solution.py
+++ b/solution.py
@@ -43,7 +43,10 @@
 
 
 def group_matrix():
-    return (np.arange(C)[:, None] // (C // GROUPS) == np.arange(GROUPS)[None, :]).astype(np.float32)
+    spread = np.zeros((4, C, 128), np.float32)
+    for quarter in range(4):
+        spread[quarter, np.arange(C), quarter * GROUPS + np.arange(C) // (C // GROUPS)] = 1.0
+    return spread
 
 
 def head_matrix():
@@ -69,31 +72,97 @@
     )(*args)
 
 
-def sums_kernel(frames, with_latent, x_ref, t_ref, g_ref, out_ref):
+def image_sums(frames, sets, x_ref, t_ref, g_ref):
     cols = x_ref.shape[0]
     count = t_ref.shape[1] // frames
     first = jnp.zeros((count, frames, C), F32)
     cross = jnp.zeros((count, frames, C), F32)
-    lat = jnp.zeros((frames, C), F32)
-    square = jnp.zeros((frames, C), F32)
     for w in range(cols):
         t = t_ref[w].astype(F32).reshape(count, frames, C)
-        x = x_ref[w]
         first = first + t
-        cross = cross + t * x[None]
-        lat = lat + x
-        square = square + x * x
-    rows = [jnp.sum(first, axis=1), jnp.sum(cross, axis=1)]
-    if with_latent:
-        rows.append(jnp.broadcast_to(jnp.sum(lat, axis=0, keepdims=True), (8, C)))
-        rows.append(jnp.broadcast_to(jnp.sum(square, axis=0, keepdims=True), (8, C)))
-    out_ref[...] = hdot(jnp.concatenate(rows, axis=0), g_ref[...])
-
-
-def latent_stats(ls_ref, members, gt):
+        cross = cross + t * x_ref[w][None]
+    first = jnp.sum(first, axis=1)
+    cross = jnp.sum(cross, axis=1)
+    half = count // sets
+    packed = jnp.zeros((half, 128), F32)
+    for k in range(sets):
+        part = slice(k * half, (k + 1) * half)
+        packed = packed + hdot(first[part], g_ref[2 * k]) + hdot(cross[part], g_ref[2 * k + 1])
+    return packed
+
+
+def input_sums_kernel(frames, x_ref, t_ref, g_ref, out_ref):
+    x = x_ref[...].reshape(-1, C)
+    lat = jnp.broadcast_to(jnp.sum(x, axis=0, keepdims=True), (8, C))
+    square = jnp.broadcast_to(jnp.sum(x * x, axis=0, keepdims=True), (8, C))
+    out_ref[0:8] = hdot(lat, g_ref[0]) + hdot(square, g_ref[1])
+    out_ref[8:] = image_sums(frames, 2, x_ref, t_ref, g_ref)
+
+
+def reduce_kernel(axes, x_ref, out_ref, slots, send_sem, recv_sem):
+    tiles, shares = lax.axis_size("tile"), lax.axis_size("probe")
+    tile, share = lax.axis_index("tile"), lax.axis_index("probe")
+    both = len(axes) == 2
+    if both:
+        count, me = tiles * shares, tile * shares + share
+    elif axes[0] == "tile":
+        count, me = tiles, tile
+    else:
+        count, me = shares, share
+
+    def device(offset):
+        other = lax.rem(me + offset, count)
+        if both:
+            return {"tile": other // shares, "probe": lax.rem(other, shares)}
+        return {axes[0]: other}
+
+    barrier = pltpu.get_barrier_semaphore()
+    for offset in range(1, count):
+        pl.semaphore_signal(
+            barrier, inc=1, device_id=device(offset), device_id_type=pl.DeviceIdType.MESH
+        )
+    pl.semaphore_wait(barrier, count - 1)
+    copies = []
+    for offset in range(1, count):
+        copy = pltpu.make_async_remote_copy(
+            src_ref=x_ref,
+            dst_ref=slots.at[me],
+            send_sem=send_sem.at[offset - 1],
+            recv_sem=recv_sem.at[offset - 1],
+            device_id=device(offset),
+            device_id_type=pl.DeviceIdType.MESH,
+        )
+        copy.start()
+        copies.append(copy)
+    slots[me] = x_ref[...]
+    for copy in copies:
+        copy.wait()
+    total = slots[0]
+    for i in range(1, count):
+        total = total + slots[i]
+    out_ref[...] = total
+
+
+def reduce_over(array, axes, collective_id):
+    count = math.prod(lax.axis_size(axis) for axis in axes)
+    return pl.pallas_call(
+        functools.partial(reduce_kernel, axes),
+        out_shape=jax.ShapeDtypeStruct(array.shape, array.dtype),
+        in_specs=[pl.BlockSpec(memory_space=pltpu.VMEM)],
+        out_specs=pl.BlockSpec(memory_space=pltpu.VMEM),
+        scratch_shapes=[
+            pltpu.VMEM((count,) + array.shape, array.dtype),
+            pltpu.SemaphoreType.DMA((count - 1,)),
+            pltpu.SemaphoreType.DMA((count - 1,)),
+        ],
+        compiler_params=pltpu.CompilerParams(collective_id=collective_id, has_side_effects=True),
+    )(array)
+
+
+def latent_stats(ls_ref, members, gt_ref):
     sums = ls_ref[...]
-    mean = sums[0:1] / members
-    inv = lax.rsqrt(sums[8:9] / members - mean * mean + EPS)
+    mean = hdot(sums, gt_ref[0])[0:1] / members
+    inv = lax.rsqrt(hdot(sums, gt_ref[1])[0:1] / members - mean * mean + EPS)
     return mean, inv
 
 
@@ -158,9 +227,7 @@
     cols, frames = x_ref.shape[0], x_ref.shape[1]
     rows = cols * frames
     hf = HEADS * frames
-    mean, inv = latent_stats(ls_ref, members, None)
-    mean = hdot(mean + jnp.zeros((8, GROUPS), F32), gt_ref[...])[0:1]
-    inv = hdot(inv + jnp.zeros((8, GROUPS), F32), gt_ref[...])[0:1]
+    mean, inv = latent_stats(ls_ref, members, gt_ref)
     gain = gain_ref[...]
     acts = []
     for r, ref in enumerate((lo_ref, x_ref, hi_ref)):
@@ -233,11 +300,11 @@
 
 def tangent_kernel(
     members,
+    which,
     lo_ref,
     t_ref,
     hi_ref,
-    first_ref,
-    cross_ref,
+    sums_ref,
     ls_ref,
     ws_ref,
     wt_ref,
@@ -259,13 +326,12 @@
     cols, frames = a_ref.shape[1], a_ref.shape[2]
     per = CHUNK * frames
     hf = HEADS * frames
-    mean, inv = latent_stats(ls_ref, members, None)
-    first = first_ref[...]
-    d_mean = first / members
-    d_var = 2.0 * (cross_ref[...] - mean * first) / members
-    d_std = -0.5 * inv * inv * inv * d_var
-    d_mean = hdot(d_mean, gt_ref[...])[:, None, :]
-    d_std = hdot(d_std, gt_ref[...])[:, None, :]
+    mean, inv = latent_stats(ls_ref, members, gt_ref)
+    first = hdot(sums_ref[...], gt_ref[2 * which])
+    cross = hdot(sums_ref[...], gt_ref[2 * which + 1])
+    d_mean = (first / members)[:, None, :]
+    d_var = 2.0 * (cross - mean * first) / members
+    d_std = (-0.5 * inv * inv * inv * d_var)[:, None, :]
     acts = []
     for r, ref in enumerate((lo_ref, t_ref, hi_ref)):
         pieces = []
@@ -317,37 +383,48 @@
     out_ref[...] = result.reshape(cols, per, C).astype(out_ref.dtype)
 
 
-def gather_rows(ref, w):
-    return jnp.concatenate([ref[p, w] for p in range(ref.shape[0])], axis=0)
-
-
-def gram_kernel(frames, s_ref, t_ref, out_ref):
+def gather_rows(ref, w, share):
+    count = ref.shape[0]
+    return jnp.concatenate(
+        [ref[lax.rem(share - p + count, count), w] for p in range(count)], axis=0
+    )
+
+
+def gram_kernel(frames, slot_ref, x_ref, own_ref, s_ref, t_ref, g_ref, out_ref):
     cols = t_ref.shape[0]
+    share = slot_ref[1]
     total = None
     for w in range(cols):
-        s = gather_rows(s_ref, w)
+        s = gather_rows(s_ref, w, share)
         term = ndot(jnp.concatenate([s, t_ref[w]], axis=0), s)
         total = term if total is None else total + term
     rows, columns = total.shape
     same = lax.rem(iota((rows, columns), 0), frames) == lax.rem(iota((rows, columns), 1), frames)
     total = jnp.where(same, total, 0.0)
     summed = jnp.sum(total.reshape(rows // frames, frames, columns), axis=1)
-    fold = jnp.where(
-        iota((columns, columns // frames), 0) // frames == iota((columns, columns // frames), 1),
-        1.0,
-        0.0,
-    )
-    out_ref[...] = hdot(summed, fold)
+    ns = columns // frames
+    packed = image_sums(frames, 1, x_ref, own_ref, g_ref)
+    own = packed.shape[0]
+    for i in range(rows // frames // own):
+        fold = jnp.where(
+            iota((columns, 128), 0) // frames + (64 + i * ns) == iota((columns, 128), 1), 1.0, 0.0
+        )
+        packed = packed + hdot(summed[i * own : (i + 1) * own], fold)
+    out_ref[...] = packed
 
 
 def combine_kernel(
-    frames, total, slot_ref, gram_ref, s_ref, js_ref, t_ref, jt_ref, basis_ref, bi_ref, ti_ref, f_ref
+    frames, ns, total, slot_ref, gram_ref, s_ref, js_ref, t_ref, jt_ref, basis_ref, bi_ref, ti_ref, f_ref
 ):
     cols = t_ref.shape[0]
-    ns = gram_ref.shape[1]
-    own = gram_ref.shape[0] - ns
-    gram = gram_ref[:ns, :]
-    cross = gram_ref[ns:, :]
+    own = gram_ref.shape[0]
+    packed = gram_ref[...]
+    pieces = []
+    for i in range(ns // own + 1):
+        choose = jnp.where(iota((128, ns), 0) == iota((128, ns), 1) + (64 + i * ns), 1.0, 0.0)
+        pieces.append(hdot(packed, choose))
+    gram = jnp.concatenate(pieces[:-1], axis=0)
+    cross = pieces[-1]
     inverse = jnp.where(iota((ns, ns), 0) == iota((ns, ns), 1), 1.0, 0.0)
     row = iota((ns, ns), 0)
     for j in range(ns):
@@ -358,6 +435,7 @@
         gram = jnp.where(row > j, gram - column * upper, gram)
         inverse = jnp.where(row > j, inverse - column * lower, jnp.where(row == j, lower, inverse))
     first = slot_ref[0]
+    share = slot_ref[1]
     pick = jnp.where(iota((own, ns), 1) == iota((own, ns), 0) + first, 1.0, 0.0)
     to_basis = math.sqrt(total) * hdot(pick, inverse)
     to_project = hdot(ndot(cross, inverse, HIGHEST), inverse)
@@ -386,8 +464,8 @@
 
     sums = [jnp.zeros((big, C), F32) for _ in range(3)]
     for w in range(cols):
-        s = gather_rows(s_ref, w)
-        js = gather_rows(js_ref, w)
+        s = gather_rows(s_ref, w, share)
+        js = gather_rows(js_ref, w, share)
         basis = apply(basis_parts, s)
         projected = t_ref[w].astype(F32) - apply(project_parts, s)
         basis_image = apply(basis_parts[:2], js)
@@ -402,7 +480,7 @@
     forms = jnp.zeros((own, 128), F32)
     for i in range(3):
         value = jnp.sum(jnp.sum(sums[i].reshape(own, frames, C), axis=1), axis=1, keepdims=True)
-        forms = jnp.where(lane == i, value, forms)
+        forms = jnp.where(lane == 4 * share + i, value, forms)
     f_ref[...] = forms
 
 
@@ -444,18 +522,18 @@
     x_lo, x_hi = neighbours(x)
     p_lo, p_hi = neighbours(p)
     group = jnp.asarray(group_matrix())
-    group_t = jnp.asarray(group_matrix().T)
+    group_t = jnp.asarray(np.swapaxes(group_matrix(), 1, 2))
     hh = jnp.asarray(head_matrix())
     hrow = jnp.asarray(head_rows())
     sums = call(
-        functools.partial(sums_kernel, frames, True),
-        jax.ShapeDtypeStruct((4 * padded + 16, GROUPS), F32),
+        functools.partial(input_sums_kernel, frames),
+        jax.ShapeDtypeStruct((8 + padded, 128), F32),
         x,
         p,
         group,
     )
-    sums = lax.psum(sums, "tile")
-    latent_sums = sums[4 * padded :]
+    sums = reduce_over(sums, ("tile",), 0)
+    latent_sums, probe_sums = sums[:8], sums[8:]
     wqkv = jnp.swapaxes(w_qkv, 0, 1)
     edge = jnp.stack([here > 0, here < tiles - 1]).astype(F32)
 
@@ -499,60 +577,50 @@
     chunks = padded // CHUNK
     per = CHUNK * frames
 
-    def tangent(lo, mid, hi, offset, first, cross, dtype):
+    def tangent(lo, mid, hi, offset, sums, which, dtype):
         fixed = (latent_sums, w_spatial, w_temporal, wqkv, w_out, group_t, hh, hrow) + tuple(caches)
         moving = pl.BlockSpec((cols, per, C), lambda i: (0, i + offset, 0))
-        stat = pl.BlockSpec((CHUNK, GROUPS), lambda i: (i, 0))
+        stat = pl.BlockSpec((CHUNK, 128), lambda i: (i, 0))
         return call(
-            functools.partial(tangent_kernel, members),
+            functools.partial(tangent_kernel, members, which),
             jax.ShapeDtypeStruct((cols, padded * frames, C), dtype),
             lo,
             mid,
             hi,
-            first,
-            cross,
+            sums,
             *fixed,
             grid=(chunks,),
-            in_specs=[moving] * 3 + [stat] * 2 + [vmem] * len(fixed),
+            in_specs=[moving] * 3 + [stat] + [vmem] * len(fixed),
             out_specs=pl.BlockSpec((cols, per, C), lambda i: (0, i, 0)),
             flops=2 * 10**9,
         )
 
-    sketch = tangent(
-        p_lo, p, p_hi, 0, sums[:padded], sums[2 * padded : 3 * padded], BF16
-    )
+    def from_shares(block):
+        blocks = [block]
+        for i in range(1, shares):
+            ring = [(j, (j + i) % shares) for j in range(shares)]
+            blocks.append(lax.ppermute(block, "probe", ring))
+        return jnp.stack(blocks)
+
+    slot = jnp.stack([first_slot, lax.axis_index("probe")]).astype(jnp.int32)
+    sketch = tangent(p_lo, p, p_hi, 0, probe_sums, 0, BF16)
     s_lo, s_hi = neighbours(sketch)
-    s_sums = call(
-        functools.partial(sums_kernel, frames, False),
-        jax.ShapeDtypeStruct((2 * padded, GROUPS), F32),
-        x,
-        sketch,
-        group,
-    )
-    s_sums = lax.psum(s_sums, "tile")
-    s_all = lax.all_gather(sketch[:, : own * frames], "probe", axis=0)
-    test = tangent(
-        p_lo,
-        p,
-        p_hi,
-        chunks,
-        sums[padded : 2 * padded],
-        sums[3 * padded : 4 * padded],
-        F32,
-    )
+    s_all = from_shares(sketch[:, : own * frames])
+    test = tangent(p_lo, p, p_hi, chunks, probe_sums, 1, F32)
     p_test = p[:, padded * frames :]
-    gram = call(
+    gram = pl.pallas_call(
         functools.partial(gram_kernel, frames),
-        jax.ShapeDtypeStruct((ns + padded, ns), F32),
-        s_all,
-        p_test,
-    )
-    gram = lax.psum(gram, "tile")
-    second = tangent(s_lo, sketch, s_hi, 0, s_sums[:padded], s_sums[padded:], BF16)
-    js_all = lax.all_gather(second[:, : own * frames], "probe", axis=0)
+        in_specs=[smem] + [vmem] * 5,
+        out_shape=jax.ShapeDtypeStruct((padded, 128), F32),
+        compiler_params=pltpu.CompilerParams(vmem_limit_bytes=56 * 2**20),
+        cost_estimate=pl.CostEstimate(flops=10**9, bytes_accessed=10**7, transcendentals=0),
+    )(slot, x, sketch, s_all, p_test, group)
+    gram = reduce_over(gram, ("tile",), 1)
+    second = tangent(s_lo, sketch, s_hi, 0, gram, 0, BF16)
+    js_all = from_shares(second[:, : own * frames])
     image = (cols, padded * frames, C)
     basis, basis_images, test_images, forms = pl.pallas_call(
-        functools.partial(combine_kernel, frames, total),
+        functools.partial(combine_kernel, frames, ns, total),
         in_specs=[smem] + [vmem] * 5,
         out_shape=[
             jax.ShapeDtypeStruct(image, F32),
@@ -562,12 +630,14 @@
         ],
         compiler_params=pltpu.CompilerParams(vmem_limit_bytes=56 * 2**20),
         cost_estimate=pl.CostEstimate(flops=10**9, bytes_accessed=10**7, transcendentals=0),
-    )(first_slot.astype(jnp.int32)[None], gram, s_all, js_all, p_test, test)
-
-    own_slots = first_slot + jnp.arange(own, dtype=jnp.int32)
-    placed = jnp.arange(ns, dtype=jnp.int32)[None, :] == own_slots[:, None]
-    placed = jnp.sum(jnp.where(placed[None], forms[:own, :3].T[:, :, None], 0.0), axis=1)
-    placed = lax.psum(placed, ("tile", "probe"))
+    )(slot, gram, s_all, js_all, p_test, test)
+
+    if tiles * shares <= 64:
+        forms = reduce_over(forms, ("tile", "probe"), 2)
+    else:
+        forms = reduce_over(reduce_over(forms, ("tile",), 2), ("probe",), 3)
+    placed = jnp.transpose(forms[:own, : 4 * shares].reshape(own, shares, 4), (2, 1, 0))
+    placed = placed.reshape(4, ns)
     rayleigh = jnp.stack([placed[0] / total, placed[1] / placed[2]])
     divergence = (jnp.sum(placed[0]) / total + jnp.sum(placed[1]) / ns) / total
 

time: 277 us -> 138 us (0.50)
  blocking collectives: 178 us -> 0 us
  Pallas kernels: 56.5 us -> 89.7 us
  local copies, waits for them, and re-layouts: 23.3 us -> 17.2 us
  waiting for transfers between devices: 0.02 us -> 5.12 us
  starting transfers between devices: 12.9 us -> 16.6 us
  other arithmetic: 1.94 us -> 5.61 us
    psum x3 -> x0, blocking collectives: 159 us -> none  [the longest x1 64.6 us: on_device(): sums = lax.psum(sums, 'tile')]
    pallas_call x1 -> x5, Pallas kernels: 6.26 us -> 41.7 us  [the longest x3 31.7 us: reduce_over(): pl.pallas_call(functools.partial(reduce_kernel, axes), out_shape=jax.Shap...]
    all_gather x2 -> x0, blocking collectives: 18.8 us -> none  [the longest x1 11.1 us: on_device(): s_all = lax.all_gather(sketch[:, :own * frames], 'probe', axis=0)]
    ppermute x0 -> x2, waiting for transfers between devices: none -> 5.11 us  [from_shares(): blocks.append(lax.ppermute(block, 'probe', ring))]
    another operation x0 -> x3, other arithmetic: none -> 3.78 us  [the longest x2 3.12 us: from_shares(): return jnp.stack(blocks)]
    ppermute x0 -> x2, starting transfers between devices: none -> 3.04 us  [from_shares(): blocks.append(lax.ppermute(block, 'probe', ring))]
    pallas_call x6 -> x4, Pallas kernels: 41.9 us -> 39.4 us  [call(): pl.pallas_call(kernel, out_shape=out_shape, compiler_params=pltpu.Compile...]
  transfers between devices with their start and end apart: 6 -> 8, of which waited for: 0 -> 1; matrix products, arithmetic and copies ran while one was open for 4% -> 7% of each run, Pallas kernels for 9% -> 36%
where the time goes in v1:
time: 138 us
  Pallas kernels  89.7 us (65%)
  local copies, waits for them, and re-layouts  17.2 us (12%)
  starting transfers between devices  16.6 us (12%)
  other arithmetic  5.61 us (4%)
  waiting for transfers between devices  5.12 us (4%)
  between operations  3.33 us (2%)
    pallas_call x4, Pallas kernels, call(): pl.pallas_call(kernel, out_shape=out_shape, compiler_params=pltpu.Compile...  39.4 us
    pallas_call x3, Pallas kernels, reduce_over(): pl.pallas_call(functools.partial(reduce_kernel, axes), out_shape=jax.Shap...  31.7 us
    ppermute x3, starting transfers between devices, neighbours(): lax.ppermute(block, 'tile', forward)  9.51 us
    pallas_call x1, Pallas kernels, on_device(): pl.pallas_call(functools.partial(primal_kernel, members), in_specs=[smem,...  8.62 us
    pallas_call x1, Pallas kernels, on_device(): pl.pallas_call(functools.partial(combine_kernel, frames, ns, total), in_s...  6.52 us
    ppermute x2, waiting for transfers between devices, from_shares(): blocks.append(lax.ppermute(block, 'probe', ring))  5.11 us
    ppermute x3, starting transfers between devices, neighbours(): lax.ppermute(block, 'tile', backward)  4.06 us
    pallas_call x1, Pallas kernels, on_device(): pl.pallas_call(functools.partial(gram_kernel, frames), in_specs=[smem] +...  3.45 us
  transfers between devices with their start and end apart: 8, of which 1 were waited for; matrix products, arithmetic and copies ran while one was open for 7% of the time, Pallas kernels for 36%

profile of v1, /device:TPU:0, one launch (start us, length us, event | category | flops | bytes accessed | tf_op | source)
XLA Modules:
  0.0 137.6 jit_solution(8032816216070286920)
XLA Ops:
  0.6 0.0 copy-start.6
  0.6 0.0 copy-start.10
  0.7 0.0 copy-start.11
  0.7 0.0 copy-start.12
  0.7 0.0 copy-start.13
  0.7 1.3 copy.29
  2.0 0.0 copy-start
  2.0 0.3 copy.30
  2.3 2.4 %collective-permute-start.2 = (bf16[4,256,320]{1,2,0:T(8,128)(2,1)S(1)}, bf16[4,256,320]{1,2,0:T(8,128)(2,1)S(1)}, u32[]{:S(2)}, u32[]{:S(2)}) collective-permute-start(bf16[4,256,320]{1,2,0:T(8,128)(2,1)S(1)} %copy.30), channel_id=1, source_target_pairs={{0,2},{2,4},{4,6},{6,8},{8,10},{10,12},{12,14},{14,16},{16,18},{18... | collective-permute-start | bytes 1966088 | tf_op jit(solution)/shard_map/ppermute | solution.py:520
  4.7 1.3 collective-permute-start.3
  6.0 0.0 copy-done.6
  6.0 0.0 copy-start.3
  6.1 5.1 %collective-permute-start = (f32[4,16,320]{2,1,0:T(8,128)S(1)}, f32[4,16,320]{2,1,0:T(8,128)S(1)}, u32[]{:S(2)}, u32[]{:S(2)}) collective-permute-start(f32[4,16,320]{2,1,0:T(8,128)S(1)} %bitcast.52), channel_id=1, source_target_pairs={{0,2},{2,4},{4,6},{6,8},{8,10},{10,12},{12,14},{14,16},{16,18},{18... | collective-permute-start | bytes 245768 | tf_op jit(solution)/shard_map/ppermute | solution.py:520
  11.2 1.3 collective-permute-start.1
  12.5 0.0 copy-done
  12.5 0.0 copy-done.3
  12.5 2.8 %shard_map.190.x_ref = f32[16,128]{1,0:T(8,128)} custom-call(f32[4,16,320]{2,1,0:T(8,128)} %bitcast.54, bf16[4,256,320]{2,1,0:T(8,128)(2,1)} %bitcast.42, f32[4,320,128]{2,1,0:T(8,128)} %constant.33.clone.g_ref), custom_call_target="tpu_custom_call" | custom-call | flops 100000000 | bytes 1392640 | tf_op jit(solution)/shard_map/pallas_call | solution.py:66
  15.2 13.2 %shard_map.191 = f32[16,128]{1,0:T(8,128)} custom-call(f32[16,128]{1,0:T(8,128)} %shard_map.190.x_ref), custom_call_target="tpu_custom_call" | custom-call | tf_op jit(solution)/shard_map/pallas_call | solution.py:148
  28.5 0.6 broadcast_in_dim.24.gain_ref
  29.1 0.0 copy-done.11
  29.1 0.6 broadcast_in_dim.25.bias_ref
  29.6 0.6 broadcast_in_dim.26.sb_ref
  30.2 0.6 broadcast_in_dim.27.tb_ref
  30.8 1.3 fusion.1
  32.1 0.7 add_convert_fusion.edge_ref
  32.8 0.0 collective-permute-done.lo_ref
  32.8 0.0 collective-permute-done.1.hi_ref
  32.8 0.6 copy-done.7
  33.4 0.0 copy-done.8
  33.4 8.6 %shard_map.192 = (bf16[4,16,320]{2,1,0:T(8,128)(2,1)}, f32[3,4,16,320]{3,2,1,0:T(8,128)}, f32[3,4,16,320]{3,2,1,0:T(8,128)}, f32[6,4,16,320]{3,2,1,0:T(8,128)}, ...) custom-call(f32[2]{0:T(128)} %add_convert_fusion.edge_ref, ...), custom_call_target="tpu_custom_call" | custom-call | flops 100000000 | bytes 10000000 | tf_op jit(solution)/shard_map/pallas_call | solution.py:542
  42.1 0.0 collective-permute-done.2
  42.1 1.2 copy.32.lo_ref
  43.2 0.0 collective-permute-done.3
  43.3 1.1 copy.33.hi_ref
  44.4 12.1 %shard_map.193.own_ref.t_ref = bf16[4,128,320]{2,1,0:T(8,128)(2,1)} custom-call(bf16[4,256,320]{2,1,0:T(8,128)(2,1)} %copy.32.lo_ref, bf16[4,256,320]{2,1,0:T(8,128)(2,1)} %bitcast.43, bf16[4,256,320]{2,1,0:T(8,128)(2,1)} %copy.33.hi_ref, f32[8,128]{1,0:T(8,128)} %get-tuple-element.48.sums_ref, f32[8,128]{1,0:T(8,128)} %get-tuple-element.49.ls_ref, ...), custom_call_target="tpu_custom_call" | custom-call | flops 2000000000 | bytes 9373696 | tf_op jit(solution)/shard_map/pallas_call | solution.py:66
  56.5 1.5 %collective-permute-start.4 = (bf16[4,128,320]{2,1,0:T(8,128)(2,1)}, bf16[4,128,320]{2,1,0:T(8,128)(2,1)S(1)}, u32[]{:S(2)}, u32[]{:S(2)}) collective-permute-start(bf16[4,128,320]{2,1,0:T(8,128)(2,1)} %shard_map.193.own_ref.t_ref), channel_id=1, source_target_pairs={{0,1},{1,0},{2,3},{3,2},{4,5},{5,4},{6,7},{7,6},{8,9},{9,8},{10,11... | collective-permute-start | bytes 983048 | tf_op jit(solution)/shard_map/ppermute | solution.py:602
  58.0 0.8 slice.33.t_ref
  58.8 2.0 %collective-permute-start.5 = (bf16[4,128,320]{2,1,0:T(8,128)(2,1)}, bf16[4,128,320]{2,1,0:T(8,128)(2,1)S(1)}, u32[]{:S(2)}, u32[]{:S(2)}) collective-permute-start(bf16[4,128,320]{2,1,0:T(8,128)(2,1)} %shard_map.193.own_ref.t_ref), channel_id=1, source_target_pairs={{0,2},{2,4},{4,6},{6,8},{8,10},{10,12},{12,14},{14,16},{16,18},{18... | collective-permute-start | bytes 983048 | tf_op jit(solution)/shard_map/ppermute | solution.py:520
  60.8 1.5 %collective-permute-start.6 = (bf16[4,128,320]{2,1,0:T(8,128)(2,1)}, bf16[4,128,320]{2,1,0:T(8,128)(2,1)S(1)}, u32[]{:S(2)}, u32[]{:S(2)}) collective-permute-start(bf16[4,128,320]{2,1,0:T(8,128)(2,1)} %shard_map.193.own_ref.t_ref), channel_id=1, source_target_pairs={{2,0},{4,2},{6,4},{8,6},{10,8},{12,10},{14,12},{16,14},{18,16},{20... | collective-permute-start | bytes 983048 | tf_op jit(solution)/shard_map/ppermute | solution.py:520
  62.3 0.7 pad_add_fusion.slot_ref
  63.0 5.1 %collective-permute-done.4 = bf16[4,128,320]{2,1,0:T(8,128)(2,1)S(1)} collective-permute-done((bf16[4,128,320]{2,1,0:T(8,128)(2,1)}, bf16[4,128,320]{2,1,0:T(8,128)(2,1)S(1)}, u32[]{:S(2)}, u32[]{:S(2)}) %collective-permute-start.4) | collective-permute-done | bytes 327712 | tf_op jit(solution)/shard_map/ppermute | solution.py:602
  68.1 2.1 %pad_maximum_fusion.s_ref = bf16[2,4,128,320]{3,2,1,0:T(8,128)(2,1)} fusion(bf16[1,4,128,320]{3,2,1,0:T(8,128)(2,1)S(1)} %bitcast.63, bf16[1,4,128,320]{3,2,1,0:T(8,128)(2,1)} %bitcast.50), kind=kLoop, calls=%fused_computation | loop fusion | flops 327680 | bytes 1310720 | tf_op jit(solution)/shard_map/stack | solution.py:603
  70.2 3.5 %shard_map.194.x_ref = f32[8,128]{1,0:T(8,128)} custom-call(s32[2]{0:T(128)} %pad_add_fusion.slot_ref, f32[4,16,320]{2,1,0:T(8,128)} %bitcast.56, bf16[4,128,320]{2,1,0:T(8,128)(2,1)} %shard_map.193.own_ref.t_ref, bf16[2,4,128,320]{3,2,1,0:T(8,128)(2,1)} %pad_maximum_fusion.s_ref, bf16[4,128,320]{2,1,0:T(8,128)(2,1)} %slice.33.t_ref, ...), custom_call_target="tpu_custom_call" | custom-call | flops 1000000000 | bytes 10000000 | tf_op jit(solution)/shard_map/pallas_call | solution.py:611
  73.6 8.6 %shard_map.195.sums_ref.gram_ref = f32[8,128]{1,0:T(8,128)} custom-call(f32[8,128]{1,0:T(8,128)} %shard_map.194.x_ref), custom_call_target="tpu_custom_call" | custom-call | tf_op jit(solution)/shard_map/pallas_call | solution.py:148
  82.2 0.0 copy-start.9
  82.2 0.0 collective-permute-done.5.lo_ref
  82.2 0.0 collective-permute-done.6.hi_ref
  82.3 0.7 copy-done.4
  83.0 0.8 copy-done.5
  83.7 12.0 %shard_map.196 = bf16[4,128,320]{2,1,0:T(8,128)(2,1)} custom-call(bf16[4,128,320]{2,1,0:T(8,128)(2,1)} %copy-done.4, bf16[4,128,320]{2,1,0:T(8,128)(2,1)} %shard_map.193.own_ref.t_ref, bf16[4,128,320]{2,1,0:T(8,128)(2,1)} %copy-done.5, f32[8,128]{1,0:T(8,128)} %shard_map.195.sums_ref.gram_ref, f32[8,128]{1,0:T(8,128)} %get-tuple-element.49.ls_ref, ...), custom_call_target="tpu_custom_call" | custom-call | flops 2000000000 | bytes 8390656 | tf_op jit(solution)/shard_map/pallas_call | solution.py:66
  95.8 1.5 %collective-permute-start.7 = (bf16[4,128,320]{2,1,0:T(8,128)(2,1)}, bf16[4,128,320]{2,1,0:T(8,128)(2,1)S(1)}, u32[]{:S(2)}, u32[]{:S(2)}) collective-permute-start(bf16[4,128,320]{2,1,0:T(8,128)(2,1)} %shard_map.196), channel_id=1, source_target_pairs={{0,1},{1,0},{2,3},{3,2},{4,5},{5,4},{6,7},{7,6},{8,9},{9,8},{10,11... | collective-permute-start | bytes 983048 | tf_op jit(solution)/shard_map/ppermute | solution.py:602
  97.3 0.6 copy.40
  97.9 12.5 %shard_map.197.jt_ref = f32[4,128,320]{2,1,0:T(8,128)} custom-call(bf16[4,256,320]{2,1,0:T(8,128)(2,1)} %copy.32.lo_ref, bf16[4,256,320]{2,1,0:T(8,128)(2,1)} %bitcast.44, bf16[4,256,320]{2,1,0:T(8,128)(2,1)} %copy.33.hi_ref, f32[8,128]{1,0:T(8,128)} %get-tuple-element.48.sums_ref, f32[8,128]{1,0:T(8,128)} %get-tuple-element.49.ls_ref, ...), custom_call_target="tpu_custom_call" | custom-call | flops 2000000000 | bytes 9373696 | tf_op jit(solution)/shard_map/pallas_call | solution.py:66
  110.4 0.0 collective-permute-done.7
  110.4 1.0 pad_maximum_fusion.1.js_ref
  111.5 6.5 %shard_map.198 = (f32[4,128,320]{2,1,0:T(8,128)}, bf16[4,128,320]{2,1,0:T(8,128)(2,1)}, bf16[4,128,320]{2,1,0:T(8,128)(2,1)}, f32[8,128]{1,0:T(8,128)}) custom-call(s32[2]{0:T(128)} %pad_add_fusion.slot_ref, f32[8,128]{1,0:T(8,128)} %shard_map.195.sums_ref.gram_ref, bf16[2,4,128,320]{3,2,1,0:T(8,128)(2,1)} %pad_maximum_fusion.s_ref, ...), custom_call_target="tpu_custom_call" | custom-call | flops 1000000000 | bytes 10000000 | tf_op jit(solution)/shard_map/pallas_call | solution.py:622
  118.0 10.0 %shard_map.199 = f32[8,128]{1,0:T(8,128)} custom-call(f32[8,128]{1,0:T(8,128)} %get-tuple-element.31.x_ref), custom_call_target="tpu_custom_call" | custom-call | tf_op jit(solution)/shard_map/pallas_call | solution.py:148
  128.0 0.7 copy.39
  128.7 0.6 slice_reduce_fusion
  130.6 0.1 div.28
  130.7 0.1 div.30
  130.8 2.5 %copy.45 = f32[4,8,16,320]{3,0,2,1:T(4,128)} copy(f32[4,8,16,320]{3,2,1,0:T(8,128)} %bitcast.58) | data formatting | bytes 1310720 | tf_op jit(solution)/shard_map/reshape | solution.py:645
  133.3 0.6 pad_maximum_fusion.2
  133.9 2.6 %copy_bitcast_fusion.1 = (bf16[8,16,1,4,320]{4,3,2,1,0:T(4,128)(2,1)}, bf16[8,16,1,4,320]{4,3,2,1,0:T(4,128)(2,1)}) fusion(bf16[4,8,16,320]{3,2,1,0:T(8,128)(2,1)} %bitcast.61, bf16[4,8,16,320]{3,2,1,0:T(8,128)(2,1)} %bitcast.60), kind=kLoop, calls=%fused_computation.3 | loop fusion | bytes 1310720 | tf_op jit(solution)/shard_map/broadcast_in_dim | solution.py:646
  (13 shorter events, 0.0 us)
Async XLA Ops:
  0.6 5.4 %copy-start.6 = (f32[16,1,4,320]{3,2,1,0:T(4,128)S(1)}, f32[16,1,4,320]{3,2,1,0:T(4,128)}, u32[]{:S(2)}) copy-start(f32[16,1,4,320]{3,2,1,0:T(4,128)} %param.15) | copy-start | bytes 245764
  0.6 27.8 %copy-start.10 = (f32[320]{0:T(512)S(1)}, f32[320]{0:T(512)}, u32[]{:S(2)}) copy-start(f32[320]{0:T(512)} %param.17) | copy-start | bytes 3844
  0.7 28.4 %copy-start.11 = (f32[320]{0:T(512)S(1)}, f32[320]{0:T(512)}, u32[]{:S(2)}) copy-start(f32[320]{0:T(512)} %param.18) | copy-start | bytes 3844
  0.7 29.0 %copy-start.12 = (f32[320]{0:T(512)S(1)}, f32[320]{0:T(512)}, u32[]{:S(2)}) copy-start(f32[320]{0:T(512)} %param.20) | copy-start | bytes 3844
  0.7 29.6 %copy-start.13 = (f32[320]{0:T(512)S(1)}, f32[320]{0:T(512)}, u32[]{:S(2)}) copy-start(f32[320]{0:T(512)} %param.22) | copy-start | bytes 3844
  2.0 10.5 %copy-start = (bf16[4,2,8,16,320]{4,3,2,1,0:T(8,128)(2,1)}, bf16[4,2,8,16,320]{4,3,2,1,0:T(8,128)(2,1)S(1)}, u32[]{:S(2)}) copy-start(bf16[4,2,8,16,320]{4,3,2,1,0:T(8,128)(2,1)S(1)} %copy.29) | copy-start | bytes 1966084
  2.3 39.8 %collective-permute-start.2 = (bf16[4,256,320]{1,2,0:T(8,128)(2,1)S(1)}, bf16[4,256,320]{1,2,0:T(8,128)(2,1)S(1)}, u32[]{:S(2)}, u32[]{:S(2)}) collective-permute-start(bf16[4,256,320]{1,2,0:T(8,128)(2,1)S(1)} %copy.30), channel_id=1, source_target_pairs={{0,2},{2,4},{4,6},{6,8},{8,10},{10,12},{12,14},{14,16},{16,18},{18... | collective-permute-start | bytes 1966088 | tf_op jit(solution)/shard_map/ppermute | solution.py:520
  4.7 38.5 %collective-permute-start.3 = (bf16[4,256,320]{1,2,0:T(8,128)(2,1)S(1)}, bf16[4,256,320]{1,2,0:T(8,128)(2,1)S(1)}, u32[]{:S(2)}, u32[]{:S(2)}) collective-permute-start(bf16[4,256,320]{1,2,0:T(8,128)(2,1)S(1)} %copy.30), channel_id=1, source_target_pairs={{2,0},{4,2},{6,4},{8,6},{10,8},{12,10},{14,12},{16,14},{18,16},{20... | collective-permute-start | bytes 1966088 | tf_op jit(solution)/shard_map/ppermute | solution.py:520
  6.0 6.4 %copy-start.3 = (f32[16,1,4,320]{3,0,2,1:T(8,128)}, f32[16,1,4,320]{3,0,2,1:T(8,128)S(1)}, u32[]{:S(2)}) copy-start(f32[16,1,4,320]{3,0,2,1:T(8,128)S(1)} %copy.46) | copy-start | bytes 245764
  6.1 26.7 %collective-permute-start = (f32[4,16,320]{2,1,0:T(8,128)S(1)}, f32[4,16,320]{2,1,0:T(8,128)S(1)}, u32[]{:S(2)}, u32[]{:S(2)}) collective-permute-start(f32[4,16,320]{2,1,0:T(8,128)S(1)} %bitcast.52), channel_id=1, source_target_pairs={{0,2},{2,4},{4,6},{6,8},{8,10},{10,12},{12,14},{14,16},{16,18},{18... | collective-permute-start | bytes 245768 | tf_op jit(solution)/shard_map/ppermute | solution.py:520
  11.2 21.6 %collective-permute-start.1 = (f32[4,16,320]{2,1,0:T(8,128)S(1)}, f32[4,16,320]{2,1,0:T(8,128)S(1)}, u32[]{:S(2)}, u32[]{:S(2)}) collective-permute-start(f32[4,16,320]{2,1,0:T(8,128)S(1)} %bitcast.53), channel_id=1, source_target_pairs={{2,0},{4,2},{6,4},{8,6},{10,8},{12,10},{14,12},{16,14},{18,16},{20... | collective-permute-start | bytes 245768 | tf_op jit(solution)/shard_map/ppermute | solution.py:520
  32.8 0.6 copy-start.7
  32.8 0.7 copy-start.8
  44.4 13.6 %copy-start.1 = (bf16[4,2,8,16,320]{4,3,2,1,0:T(8,128)(2,1)S(1)}, bf16[4,2,8,16,320]{4,3,2,1,0:T(8,128)(2,1)}, u32[]{:S(2)}) copy-start(bf16[4,2,8,16,320]{4,3,2,1,0:T(8,128)(2,1)} %copy-done) | copy-start | bytes 1966084
  56.5 11.6 %collective-permute-start.4 = (bf16[4,128,320]{2,1,0:T(8,128)(2,1)}, bf16[4,128,320]{2,1,0:T(8,128)(2,1)S(1)}, u32[]{:S(2)}, u32[]{:S(2)}) collective-permute-start(bf16[4,128,320]{2,1,0:T(8,128)(2,1)} %shard_map.193.own_ref.t_ref), channel_id=1, source_target_pairs={{0,1},{1,0},{2,3},{3,2},{4,5},{5,4},{6,7},{7,6},{8,9},{9,8},{10,11... | collective-permute-start | bytes 983048 | tf_op jit(solution)/shard_map/ppermute | solution.py:602
  58.8 23.4 %collective-permute-start.5 = (bf16[4,128,320]{2,1,0:T(8,128)(2,1)}, bf16[4,128,320]{2,1,0:T(8,128)(2,1)S(1)}, u32[]{:S(2)}, u32[]{:S(2)}) collective-permute-start(bf16[4,128,320]{2,1,0:T(8,128)(2,1)} %shard_map.193.own_ref.t_ref), channel_id=1, source_target_pairs={{0,2},{2,4},{4,6},{6,8},{8,10},{10,12},{12,14},{14,16},{16,18},{18... | collective-permute-start | bytes 983048 | tf_op jit(solution)/shard_map/ppermute | solution.py:520
  60.8 21.4 %collective-permute-start.6 = (bf16[4,128,320]{2,1,0:T(8,128)(2,1)}, bf16[4,128,320]{2,1,0:T(8,128)(2,1)S(1)}, u32[]{:S(2)}, u32[]{:S(2)}) collective-permute-start(bf16[4,128,320]{2,1,0:T(8,128)(2,1)} %shard_map.193.own_ref.t_ref), channel_id=1, source_target_pairs={{2,0},{4,2},{6,4},{8,6},{10,8},{12,10},{14,12},{16,14},{18,16},{20... | collective-permute-start | bytes 983048 | tf_op jit(solution)/shard_map/ppermute | solution.py:520
  82.2 15.1 %copy-start.9 = (bf16[4,16,320]{2,1,0:T(8,128)(2,1)S(1)}, bf16[4,16,320]{2,1,0:T(8,128)(2,1)}, u32[]{:S(2)}) copy-start(bf16[4,16,320]{2,1,0:T(8,128)(2,1)} %get-tuple-element.19) | copy-start | bytes 122884
  82.2 0.7 copy-start.4
  83.0 0.8 copy-start.5
  95.8 14.6 %collective-permute-start.7 = (bf16[4,128,320]{2,1,0:T(8,128)(2,1)}, bf16[4,128,320]{2,1,0:T(8,128)(2,1)S(1)}, u32[]{:S(2)}, u32[]{:S(2)}) collective-permute-start(bf16[4,128,320]{2,1,0:T(8,128)(2,1)} %shard_map.196), channel_id=1, source_target_pairs={{0,1},{1,0},{2,3},{3,2},{4,5},{5,4},{6,7},{7,6},{8,9},{9,8},{10,11... | collective-permute-start | bytes 983048 | tf_op jit(solution)/shard_map/ppermute | solution.py:602
  97.9 12.5 %copy-start.2 = (bf16[4,128,320]{2,1,0:T(8,128)(2,1)S(1)}, bf16[4,128,320]{2,1,0:T(8,128)(2,1)}, u32[]{:S(2)}) copy-start(bf16[4,128,320]{2,1,0:T(8,128)(2,1)} %shard_map.196) | copy-start | bytes 983044

commit v2 on v1

--- a/solution.py
+++ b/solution.py
@@ -91,12 +91,176 @@
     return packed
 
 
-def input_sums_kernel(frames, x_ref, t_ref, g_ref, out_ref):
+MESH = pl.DeviceIdType.MESH
+
+
+class Halo:
+    def __init__(self, tile, tiles, sources, lows, highs, send_sem, recv_sem):
+        self.tile, self.tiles = tile, tiles
+        self.up, self.down = [], []
+        for i, (source, low, high) in enumerate(zip(sources, lows, highs)):
+            for copies, target, place, slot in (
+                (self.up, low, lax.rem(tile + 1, tiles), 2 * i),
+                (self.down, high, lax.rem(tile + tiles - 1, tiles), 2 * i + 1),
+            ):
+                copies.append(
+                    pltpu.make_async_remote_copy(
+                        src_ref=source,
+                        dst_ref=target,
+                        send_sem=send_sem.at[slot],
+                        recv_sem=recv_sem.at[slot],
+                        device_id={"tile": place},
+                        device_id_type=MESH,
+                    )
+                )
+
+    def start(self):
+        @pl.when(self.tile < self.tiles - 1)
+        def _():
+            for copy in self.up:
+                copy.start()
+
+        @pl.when(self.tile > 0)
+        def _():
+            for copy in self.down:
+                copy.start()
+
+    def wait(self):
+        @pl.when(self.tile < self.tiles - 1)
+        def _():
+            for copy in self.up:
+                copy.wait_send()
+            for copy in self.down:
+                copy.wait_recv()
+
+        @pl.when(self.tile > 0)
+        def _():
+            for copy in self.down:
+                copy.wait_send()
+            for copy in self.up:
+                copy.wait_recv()
+
+
+def tile_sends(tile, tiles, source, slots, send_sem, recv_sem):
+    return [
+        pltpu.make_async_remote_copy(
+            src_ref=source,
+            dst_ref=slots.at[tile],
+            send_sem=send_sem.at[offset - 1],
+            recv_sem=recv_sem.at[offset - 1],
+            device_id={"tile": lax.rem(tile + offset, tiles)},
+            device_id_type=MESH,
+        )
+        for offset in range(1, tiles)
+    ]
+
+
+def signal_peers(axis, me, count):
+    barrier = pltpu.get_barrier_semaphore()
+    for offset in range(1, count):
+        pl.semaphore_signal(
+            barrier, inc=1, device_id={axis: lax.rem(me + offset, count)}, device_id_type=MESH
+        )
+
+
+def add_slots(slots):
+    total = slots[0]
+    for i in range(1, slots.shape[0]):
+        total = total + slots[i]
+    return total
+
+
+def input_kernel(
+    frames,
+    x_ref,
+    t_ref,
+    g_ref,
+    out_ref,
+    x_lo,
+    x_hi,
+    t_lo,
+    t_hi,
+    mine,
+    slots,
+    send_sem,
+    recv_sem,
+    halo_send,
+    halo_recv,
+):
+    tiles, tile = lax.axis_size("tile"), lax.axis_index("tile")
+    signal_peers("tile", tile, tiles)
     x = x_ref[...].reshape(-1, C)
     lat = jnp.broadcast_to(jnp.sum(x, axis=0, keepdims=True), (8, C))
     square = jnp.broadcast_to(jnp.sum(x * x, axis=0, keepdims=True), (8, C))
-    out_ref[0:8] = hdot(lat, g_ref[0]) + hdot(square, g_ref[1])
-    out_ref[8:] = image_sums(frames, 2, x_ref, t_ref, g_ref)
+    mine[0:8] = hdot(lat, g_ref[0]) + hdot(square, g_ref[1])
+    mine[8:] = image_sums(frames, 2, x_ref, t_ref, g_ref)
+    slots[tile] = mine[...]
+    pl.semaphore_wait(pltpu.get_barrier_semaphore(), tiles - 1)
+    halo = Halo(tile, tiles, (x_ref, t_ref), (x_lo, t_lo), (x_hi, t_hi), halo_send, halo_recv)
+    sends = tile_sends(tile, tiles, mine, slots, send_sem, recv_sem)
+    for copy in sends:
+        copy.start()
+    halo.start()
+    for copy in sends:
+        copy.wait()
+    out_ref[...] = add_slots(slots)
+    halo.wait()
+
+
+def sketch_kernel(
+    frames,
+    own,
+    x_ref,
+    s_ref,
+    t_ref,
+    g_ref,
+    out_ref,
+    s_all,
+    s_lo,
+    s_hi,
+    mine,
+    slots,
+    send_sem,
+    recv_sem,
+    halo_send,
+    halo_recv,
+    share_send,
+    share_recv,
+):
+    tiles, tile = lax.axis_size("tile"), lax.axis_index("tile")
+    shares, share = lax.axis_size("probe"), lax.axis_index("probe")
+    signal_peers("tile", tile, tiles)
+    signal_peers("probe", share, shares)
+    s_all[0] = s_ref[:, : own * frames]
+    pl.semaphore_wait(pltpu.get_barrier_semaphore(), tiles + shares - 2)
+    source = s_ref if own * frames == s_ref.shape[1] else s_ref.at[:, : own * frames]
+    gathers = [
+        pltpu.make_async_remote_copy(
+            src_ref=source,
+            dst_ref=s_all.at[i],
+            send_sem=share_send.at[i - 1],
+            recv_sem=share_recv.at[i - 1],
+            device_id={"probe": lax.rem(share + i, shares)},
+            device_id_type=MESH,
+        )
+        for i in range(1, shares)
+    ]
+    for copy in gathers:
+        copy.start()
+    halo = Halo(tile, tiles, (s_ref,), (s_lo,), (s_hi,), halo_send, halo_recv)
+    halo.start()
+    packed = image_sums(frames, 1, x_ref, s_ref, g_ref)
+    for copy in gathers:
+        copy.wait()
+    mine[...] = packed + pack_gram(frames, share, s_all, t_ref, packed.shape[0])
+    slots[tile] = mine[...]
+    sends = tile_sends(tile, tiles, mine, slots, send_sem, recv_sem)
+    for copy in sends:
+        copy.start()
+    for copy in sends:
+        copy.wait()
+    out_ref[...] = add_slots(slots)
+    halo.wait()
 
 
 def reduce_kernel(axes, x_ref, out_ref, slots, send_sem, recv_sem):
@@ -166,6 +330,11 @@
     return mean, inv
 
 
+def inside(r):
+    tile = lax.axis_index("tile")
+    return tile > 0 if r == 0 else tile < lax.axis_size("tile") - 1
+
+
 def conv_rows(act, w_ref, cols, per):
     total = None
     left = None
@@ -198,16 +367,12 @@
 
 def primal_kernel(
     members,
-    edge_ref,
     temper_ref,
     lo_ref,
     x_ref,
     hi_ref,
     ls_ref,
-    gain_ref,
-    bias_ref,
-    sb_ref,
-    tb_ref,
+    vec_ref,
     ws_ref,
     wt_ref,
     wqkv_ref,
@@ -228,23 +393,26 @@
     rows = cols * frames
     hf = HEADS * frames
     mean, inv = latent_stats(ls_ref, members, gt_ref)
-    gain = gain_ref[...]
+    gain = vec_ref[0:1]
     acts = []
     for r, ref in enumerate((lo_ref, x_ref, hi_ref)):
-        centered = ref[...].reshape(rows, C) - mean
-        normed = centered * inv * gain + bias_ref[...]
+        value = ref[...].reshape(rows, C)
+        if r != 1:
+            value = jnp.where(inside(r), value, 0.0)
+        centered = value - mean
+        normed = centered * inv * gain + vec_ref[1:2]
         sig = jax.nn.sigmoid(normed)
         slope = sig * (1.0 + normed * (1.0 - sig)) * gain
         active = normed * sig
         if r != 1:
-            keep = edge_ref[r // 2]
+            keep = jnp.where(inside(r), 1.0, 0.0)
             slope = slope * keep
             active = active * keep
         a_ref[r] = (slope * inv).reshape(cols, frames, C)
         b_ref[r] = (slope * centered).reshape(cols, frames, C)
         acts.append(active.astype(BF16))
-    spatial = (conv_rows(acts, ws_ref, cols, frames) + sb_ref[...]).astype(BF16)
-    residual = x_ref[...].reshape(rows, C) + tb_ref[...] + conv_frames(spatial, wt_ref, frames)
+    spatial = (conv_rows(acts, ws_ref, cols, frames) + vec_ref[2:3]).astype(BF16)
+    residual = x_ref[...].reshape(rows, C) + vec_ref[3:4] + conv_frames(spatial, wt_ref, frames)
     rounded = residual.astype(BF16)
     q = dot(rounded, wqkv_ref[0])
     k = dot(rounded, wqkv_ref[1])
@@ -337,6 +505,8 @@
         pieces = []
         for w in range(cols):
             t = ref[w].astype(F32).reshape(CHUNK, frames, C)
+            if r != 1:
+                t = jnp.where(inside(r), t, 0.0)
             piece = a_ref[r, w][None] * (t - d_mean) + b_ref[r, w][None] * d_std
             pieces.append(piece.reshape(per, C).astype(BF16))
         acts.append(jnp.concatenate(pieces, axis=0))
@@ -390,31 +560,30 @@
     )
 
 
-def gram_kernel(frames, slot_ref, x_ref, own_ref, s_ref, t_ref, g_ref, out_ref):
+def pack_gram(frames, share, s_ref, t_ref, own):
     cols = t_ref.shape[0]
-    share = slot_ref[1]
+    half = t_ref.shape[1] // 2
     total = None
     for w in range(cols):
         s = gather_rows(s_ref, w, share)
-        term = ndot(jnp.concatenate([s, t_ref[w]], axis=0), s)
+        term = ndot(jnp.concatenate([s, t_ref[w, half:]], axis=0), s)
         total = term if total is None else total + term
     rows, columns = total.shape
     same = lax.rem(iota((rows, columns), 0), frames) == lax.rem(iota((rows, columns), 1), frames)
     total = jnp.where(same, total, 0.0)
     summed = jnp.sum(total.reshape(rows // frames, frames, columns), axis=1)
     ns = columns // frames
-    packed = image_sums(frames, 1, x_ref, own_ref, g_ref)
-    own = packed.shape[0]
+    packed = jnp.zeros((own, 128), F32)
     for i in range(rows // frames // own):
         fold = jnp.where(
             iota((columns, 128), 0) // frames + (64 + i * ns) == iota((columns, 128), 1), 1.0, 0.0
         )
         packed = packed + hdot(summed[i * own : (i + 1) * own], fold)
-    out_ref[...] = packed
+    return packed
 
 
 def combine_kernel(
-    frames, ns, total, slot_ref, gram_ref, s_ref, js_ref, t_ref, jt_ref, basis_ref, bi_ref, ti_ref, f_ref
+    frames, ns, count, total, gram_ref, s_ref, js_ref, t_ref, jt_ref, basis_ref, bi_ref, ti_ref, f_ref
 ):
     cols = t_ref.shape[0]
     own = gram_ref.shape[0]
@@ -434,8 +603,8 @@
         lower = inverse[j : j + 1, :] * scale
         gram = jnp.where(row > j, gram - column * upper, gram)
         inverse = jnp.where(row > j, inverse - column * lower, jnp.where(row == j, lower, inverse))
-    first = slot_ref[0]
-    share = slot_ref[1]
+    share = lax.axis_index("probe")
+    first = share * count
     pick = jnp.where(iota((own, ns), 1) == iota((own, ns), 0) + first, 1.0, 0.0)
     to_basis = math.sqrt(total) * hdot(pick, inverse)
     to_project = hdot(ndot(cross, inverse, HIGHEST), inverse)
@@ -467,7 +636,7 @@
         s = gather_rows(s_ref, w, share)
         js = gather_rows(js_ref, w, share)
         basis = apply(basis_parts, s)
-        projected = t_ref[w].astype(F32) - apply(project_parts, s)
+        projected = t_ref[w, t_ref.shape[1] // 2 :].astype(F32) - apply(project_parts, s)
         basis_image = apply(basis_parts[:2], js)
         test_image = jt_ref[w] - apply(project_parts[:2], js)
         basis_ref[w] = basis
@@ -505,43 +674,61 @@
     total = latent.size * tiles
     members = total // GROUPS
     hf = HEADS * frames
-    here = lax.axis_index("tile")
-    first_slot = lax.axis_index("probe") * own
 
     x = jnp.swapaxes(latent[:, 0], 0, 1)
     p = jnp.transpose(probes[:, :, :, 0], (3, 0, 1, 2, 4))
     if padded != own:
         p = jnp.pad(p, ((0, 0), (0, 0), (0, padded - own), (0, 0), (0, 0)))
     p = p.reshape(cols, 2 * padded * frames, C)
-    forward = [(i, i + 1) for i in range(tiles - 1)]
-    backward = [(j, i) for i, j in forward]
-
-    def neighbours(block):
-        return lax.ppermute(block, "tile", forward), lax.ppermute(block, "tile", backward)
-
-    x_lo, x_hi = neighbours(x)
-    p_lo, p_hi = neighbours(p)
     group = jnp.asarray(group_matrix())
     group_t = jnp.asarray(np.swapaxes(group_matrix(), 1, 2))
     hh = jnp.asarray(head_matrix())
     hrow = jnp.asarray(head_rows())
-    sums = call(
-        functools.partial(input_sums_kernel, frames),
-        jax.ShapeDtypeStruct((8 + padded, 128), F32),
-        x,
-        p,
-        group,
-    )
-    sums = reduce_over(sums, ("tile",), 0)
+    smem = pl.BlockSpec(memory_space=pltpu.SMEM)
+    vmem = pl.BlockSpec(memory_space=pltpu.VMEM)
+    anywhere = pl.BlockSpec(memory_space=pl.ANY)
+
+    def like(array):
+        return jax.ShapeDtypeStruct(array.shape, array.dtype)
+
+    def exchange(kernel, args, outs, out_specs, rows, halos, collective_id, extra=()):
+        block = (rows, 128)
+        semaphores = pltpu.SemaphoreType.DMA
+        return pl.pallas_call(
+            kernel,
+            in_specs=[vmem] * len(args),
+            out_shape=[jax.ShapeDtypeStruct(block, F32)] + outs,
+            out_specs=[vmem] + out_specs,
+            scratch_shapes=[
+                pltpu.VMEM(block, F32),
+                pltpu.VMEM((tiles,) + block, F32),
+                semaphores((tiles - 1,)),
+                semaphores((tiles - 1,)),
+                semaphores((2 * halos,)),
+                semaphores((2 * halos,)),
+            ]
+            + [semaphores(shape) for shape in extra],
+            compiler_params=pltpu.CompilerParams(
+                collective_id=collective_id,
+                has_side_effects=True,
+                vmem_limit_bytes=40 * 2**20,
+            ),
+        )(*args)
+
+    sums, x_lo, x_hi, p_lo, p_hi = exchange(
+        functools.partial(input_kernel, frames),
+        (x, p, group),
+        [like(x), like(x), like(p), like(p)],
+        [anywhere] * 4,
+        8 + padded,
+        2,
+        0,
+    )
     latent_sums, probe_sums = sums[:8], sums[8:]
     wqkv = jnp.swapaxes(w_qkv, 0, 1)
-    edge = jnp.stack([here > 0, here < tiles - 1]).astype(F32)
-
-    smem = pl.BlockSpec(memory_space=pltpu.SMEM)
-    vmem = pl.BlockSpec(memory_space=pltpu.VMEM)
     primal = pl.pallas_call(
         functools.partial(primal_kernel, members),
-        in_specs=[smem, smem] + [vmem] * 14,
+        in_specs=[smem] + [vmem] * 11,
         out_shape=[
             jax.ShapeDtypeStruct((cols, frames, C), BF16),
             jax.ShapeDtypeStruct((3, cols, frames, C), F32),
@@ -556,16 +743,12 @@
         compiler_params=pltpu.CompilerParams(vmem_limit_bytes=56 * 2**20),
         cost_estimate=pl.CostEstimate(flops=10**8, bytes_accessed=10**7, transcendentals=0),
     )(
-        edge,
         temper,
         x_lo,
         x,
         x_hi,
         latent_sums,
-        gn_gain[None],
-        gn_bias[None],
-        spatial_bias[None],
-        temporal_bias[None],
+        jnp.stack([gn_gain, gn_bias, spatial_bias, temporal_bias]),
         w_spatial,
         w_temporal,
         wqkv,
@@ -602,26 +785,24 @@
             blocks.append(lax.ppermute(block, "probe", ring))
         return jnp.stack(blocks)
 
-    slot = jnp.stack([first_slot, lax.axis_index("probe")]).astype(jnp.int32)
     sketch = tangent(p_lo, p, p_hi, 0, probe_sums, 0, BF16)
-    s_lo, s_hi = neighbours(sketch)
-    s_all = from_shares(sketch[:, : own * frames])
+    gram, s_all, s_lo, s_hi = exchange(
+        functools.partial(sketch_kernel, frames, own),
+        (x, sketch, p, group),
+        [jax.ShapeDtypeStruct((shares, cols, own * frames, C), BF16), like(sketch), like(sketch)],
+        [vmem, anywhere, anywhere],
+        padded,
+        1,
+        1,
+        [(shares - 1,), (shares - 1,)],
+    )
     test = tangent(p_lo, p, p_hi, chunks, probe_sums, 1, F32)
-    p_test = p[:, padded * frames :]
-    gram = pl.pallas_call(
-        functools.partial(gram_kernel, frames),
-        in_specs=[smem] + [vmem] * 5,
-        out_shape=jax.ShapeDtypeStruct((padded, 128), F32),
-        compiler_params=pltpu.CompilerParams(vmem_limit_bytes=56 * 2**20),
-        cost_estimate=pl.CostEstimate(flops=10**9, bytes_accessed=10**7, transcendentals=0),
-    )(slot, x, sketch, s_all, p_test, group)
-    gram = reduce_over(gram, ("tile",), 1)
     second = tangent(s_lo, sketch, s_hi, 0, gram, 0, BF16)
     js_all = from_shares(second[:, : own * frames])
     image = (cols, padded * frames, C)
     basis, basis_images, test_images, forms = pl.pallas_call(
-        functools.partial(combine_kernel, frames, ns, total),
-        in_specs=[smem] + [vmem] * 5,
+        functools.partial(combine_kernel, frames, ns, own, total),
+        in_specs=[vmem] * 5,
         out_shape=[
             jax.ShapeDtypeStruct(image, F32),
             jax.ShapeDtypeStruct(image, BF16),
@@ -630,7 +811,7 @@
         ],
         compiler_params=pltpu.CompilerParams(vmem_limit_bytes=56 * 2**20),
         cost_estimate=pl.CostEstimate(flops=10**9, bytes_accessed=10**7, transcendentals=0),
-    )(slot, gram, s_all, js_all, p_test, test)
+    )(gram, s_all, js_all, p, test)
 
     if tiles * shares <= 64:
         forms = reduce_over(forms, ("tile", "probe"), 2)

time: 138 us -> 135 us (0.978)
  Pallas kernels: 89.7 us -> 108 us
  starting transfers between devices: 16.6 us -> 0.51 us
  waiting for transfers between devices: 5.12 us -> 0.01 us
  other arithmetic: 5.61 us -> 2.82 us
  local copies, waits for them, and re-layouts: 17.2 us -> 19.3 us
    pallas_call x3 -> x4, Pallas kernels: 18.6 us -> 62.2 us  [the longest x2 47 us: exchange(): pl.pallas_call(kernel, in_specs=[vmem] * len(args), out_shape=[jax.ShapeD...]
    pallas_call x3 -> x1, Pallas kernels: 31.7 us -> 9.52 us  [reduce_over(): pl.pallas_call(functools.partial(reduce_kernel, axes), out_shape=jax.Shap...]
    ppermute x6 -> x0, starting transfers between devices: 13.6 us -> none  [the longest x3 9.51 us: neighbours(): lax.ppermute(block, 'tile', forward)]
    unnamed x30 -> x34, local copies, waits for them, and re-layouts: 2.82 us -> 8.57 us
    ppermute x2 -> x1, waiting for transfers between devices: 5.11 us -> 0.01 us  [from_shares(): blocks.append(lax.ppermute(block, 'probe', ring))]
    another operation x0 -> x4, local copies, waits for them, and re-layouts: none -> 2.8 us  [on_device(): jnp.stack([gn_gain, gn_bias, spatial_bias, temporal_bias])]
    pallas_call x4 -> x3, Pallas kernels: 39.4 us -> 36.6 us  [call(): pl.pallas_call(kernel, out_shape=out_shape, compiler_params=pltpu.Compile...]
    ppermute x2 -> x1, starting transfers between devices: 3.04 us -> 0.51 us  [from_shares(): blocks.append(lax.ppermute(block, 'probe', ring))]
  transfers between devices with their start and end apart: 8 -> 1, of which waited for: 1 -> 0; matrix products, arithmetic and copies ran while one was open for 7% -> 0% of each run, Pallas kernels for 36% -> 9%
where the time goes in v2:
time: 135 us; the launch traced here: 134 us
  Pallas kernels  108 us (80%)
  local copies, waits for them, and re-layouts  19.3 us (14%)
  between operations  3.21 us (2%)
  other arithmetic  2.82 us (2%)
    pallas_call x2, Pallas kernels, exchange(): pl.pallas_call(kernel, in_specs=[vmem] * len(args), out_shape=[jax.ShapeD...  47 us
    pallas_call x3, Pallas kernels, call(): pl.pallas_call(kernel, out_shape=out_shape, compiler_params=pltpu.Compile...  36.6 us
    pallas_call x1, Pallas kernels, reduce_over(): pl.pallas_call(functools.partial(reduce_kernel, axes), out_shape=jax.Shap...  9.52 us
    pallas_call x1, Pallas kernels, on_device(): pl.pallas_call(functools.partial(primal_kernel, members), in_specs=[smem]...  8.57 us
    unnamed x34, local copies, waits for them, and re-layouts  8.57 us
    pallas_call x1, Pallas kernels, on_device(): pl.pallas_call(functools.partial(combine_kernel, frames, ns, own, total),...  6.65 us
    another operation x4, local copies, waits for them, and re-layouts, on_device(): jnp.stack([gn_gain, gn_bias, spatial_bias, temporal_bias])  2.8 us
  transfers between devices with their start and end apart: 1, of which 0 were waited for; matrix products, arithmetic and copies ran while one was open for 0% of the time, Pallas kernels for 9%

profile of v2, /device:TPU:0, one launch (start us, length us, event | category | flops | bytes accessed | tf_op | source)
XLA Modules:
  0.0 134.2 jit_solution(10826775815988767297)
XLA Ops:
  0.6 0.0 copy-start.5
  0.6 0.7 stack.29
  1.4 0.7 stack.30
  2.1 0.7 stack.31
  2.8 0.7 stack.32
  3.4 0.9 copy.33
  4.3 0.0 copy-start.6
  4.3 1.3 copy.22
  5.6 0.0 copy-start
  5.6 0.0 copy-done.5
  5.6 9.5 %shard_map.190 = (f32[16,128]{1,0:T(8,128)S(1)}, f32[4,16,320]{2,1,0:T(8,128)S(1)}, f32[4,16,320]{2,1,0:T(8,128)S(1)}, bf16[4,256,320]{2,1,0:T(8,128)(2,1)S(1)}, bf16[4,256,320]{2,1,0:T(8,128)(2,1)S(1)}) custom-call(f32[4,16,320]{2,1,0:T(8,128)S(1)} %bitcast.40, bf16[4,256,320]{2,1,0:T(8,128)(2,1)S(1)} %bitcast.35, f32[4,320,128]{2,1,0:T(8,128)S(1)} %copy-done.5), custom_call_target="tpu_custom_call" | custom-call | tf_op jit(solution)/shard_map/pallas_call | solution.py:697
  15.1 0.0 copy-start.3
  15.1 0.9 copy-done.3
  16.0 0.0 copy-start.4
  16.0 0.9 copy-done.4
  16.9 0.0 copy-start.10
  16.9 0.6 copy-done.10
  17.6 0.0 copy-start.11
  17.6 0.6 copy-done.11
  18.2 0.6 fusion.1
  18.8 0.6 pad_maximum_fusion.1.vec_ref
  19.4 0.0 copy-done.6
  19.4 8.6 %shard_map.191 = (bf16[4,16,320]{2,1,0:T(8,128)(2,1)}, f32[3,4,16,320]{3,2,1,0:T(8,128)}, f32[3,4,16,320]{3,2,1,0:T(8,128)}, f32[6,4,16,320]{3,2,1,0:T(8,128)}, ...) custom-call(f32[8]{0:T(128)} %temper_ref.1, ...), custom_call_target="tpu_custom_call" | custom-call | flops 100000000 | bytes 10000000 | tf_op jit(solution)/shard_map/pallas_call | solution.py:729
  28.0 0.0 copy-done
  28.0 0.0 copy-start.1
  28.0 0.0 copy-start.7
  28.0 12.1 %shard_map.192.s_ref.t_ref = bf16[4,128,320]{2,1,0:T(8,128)(2,1)} custom-call(bf16[4,256,320]{2,1,0:T(8,128)(2,1)} %copy-done.3, bf16[4,256,320]{2,1,0:T(8,128)(2,1)} %bitcast.36, bf16[4,256,320]{2,1,0:T(8,128)(2,1)} %copy-done.4, f32[8,128]{1,0:T(8,128)} %get-tuple-element.60.sums_ref, f32[8,128]{1,0:T(8,128)} %get-tuple-element.61.ls_ref, ...), custom_call_target="tpu_custom_call" | custom-call | flops 2000000000 | bytes 9373696 | tf_op jit(solution)/shard_map/pallas_call | solution.py:66
  40.1 0.0 copy-done.1
  40.1 0.0 copy-done.7
  40.1 0.0 copy-start.2
  40.1 1.0 copy-done.2
  41.1 37.5 %shard_map.193 = (f32[8,128]{1,0:T(8,128)S(1)}, bf16[2,4,128,320]{3,2,1,0:T(8,128)(2,1)S(1)}, bf16[4,128,320]{2,1,0:T(8,128)(2,1)S(1)}, bf16[4,128,320]{2,1,0:T(8,128)(2,1)S(1)}) custom-call(f32[4,16,320]{2,1,0:T(8,128)S(1)} %bitcast.42, bf16[4,128,320]{2,1,0:T(8,128)(2,1)S(1)} %copy-done.2, bf16[4,256,320]{2,1,0:T(8,128)(2,1)S(1)} %bitcast.39, ...), custom_call_target="tpu_custom_call" | custom-call | tf_op jit(solution)/shard_map/pallas_call | solution.py:697
  78.7 0.0 copy-start.8
  78.7 0.7 copy-done.8
  79.4 0.0 copy-start.9
  79.4 0.7 copy-done.9
  80.2 0.0 copy-start.12
  80.2 0.6 copy-done.12
  80.8 0.0 copy-start.13
  80.8 0.9 copy-done.13
  81.6 0.0 copy-start.15
  81.7 12.0 %shard_map.194 = bf16[4,128,320]{2,1,0:T(8,128)(2,1)} custom-call(bf16[4,128,320]{2,1,0:T(8,128)(2,1)} %copy-done.8, bf16[4,128,320]{2,1,0:T(8,128)(2,1)} %shard_map.192.s_ref.t_ref, bf16[4,128,320]{2,1,0:T(8,128)(2,1)} %copy-done.9, f32[8,128]{1,0:T(8,128)} %copy-done.12, f32[8,128]{1,0:T(8,128)} %get-tuple-element.61.ls_ref, bf16[9,320,320]{2,1,0:T(8,128)(2,1)} %ws_ref.7, ...), custom_call_target="tpu_custom_call" | custom-call | flops 2000000000 | bytes 8390656 | tf_op jit(solution)/shard_map/pallas_call | solution.py:66
  93.7 0.5 collective-permute-start
  94.2 0.0 copy-done.15
  94.2 0.6 copy.27
  94.8 0.0 copy-start.14
  94.9 12.5 %shard_map.195.jt_ref = f32[4,128,320]{2,1,0:T(8,128)} custom-call(bf16[4,256,320]{2,1,0:T(8,128)(2,1)} %copy-done.3, bf16[4,256,320]{2,1,0:T(8,128)(2,1)} %bitcast.37, bf16[4,256,320]{2,1,0:T(8,128)(2,1)} %copy-done.4, f32[8,128]{1,0:T(8,128)} %get-tuple-element.60.sums_ref, f32[8,128]{1,0:T(8,128)} %get-tuple-element.61.ls_ref, ...), custom_call_target="tpu_custom_call" | custom-call | flops 2000000000 | bytes 9373696 | tf_op jit(solution)/shard_map/pallas_call | solution.py:66
  107.3 0.0 collective-permute-done
  107.3 0.0 copy-done.14
  107.3 1.0 pad_maximum_fusion.js_ref
  108.4 6.6 %shard_map.196 = (f32[4,128,320]{2,1,0:T(8,128)}, bf16[4,128,320]{2,1,0:T(8,128)(2,1)}, bf16[4,128,320]{2,1,0:T(8,128)(2,1)}, f32[8,128]{1,0:T(8,128)}) custom-call(f32[8,128]{1,0:T(8,128)} %copy-done.12, bf16[2,4,128,320]{3,2,1,0:T(8,128)(2,1)} %copy-done.13, bf16[2,4,128,320]{3,2,1,0:T(8,128)(2,1)} %pad_maximum_fusion.js_ref, ...), custom_call_target="tpu_custom_call" | custom-call | flops 1000000000 | bytes 10000000 | tf_op jit(solution)/shard_map/pallas_call | solution.py:803
  115.0 2.5 %copy.32 = f32[4,8,16,320]{3,0,2,1:T(4,128)} copy(f32[4,8,16,320]{3,2,1,0:T(8,128)} %bitcast.50) | data formatting | bytes 1310720 | tf_op jit(solution)/shard_map/reshape | solution.py:826
  117.5 9.5 %shard_map.197 = f32[8,128]{1,0:T(8,128)} custom-call(f32[8,128]{1,0:T(8,128)} %get-tuple-element.49.x_ref), custom_call_target="tpu_custom_call" | custom-call | tf_op jit(solution)/shard_map/pallas_call | solution.py:312
  127.1 0.7 copy.26
  127.8 0.6 slice_reduce_fusion
  129.7 0.1 div.30
  129.8 0.1 div.28
  129.9 2.6 %copy_bitcast_fusion.1 = (bf16[8,16,1,4,320]{4,3,2,1,0:T(4,128)(2,1)}, bf16[8,16,1,4,320]{4,3,2,1,0:T(4,128)(2,1)}) fusion(bf16[4,8,16,320]{3,2,1,0:T(8,128)(2,1)} %bitcast.52, bf16[4,8,16,320]{3,2,1,0:T(8,128)(2,1)} %bitcast.51), kind=kLoop, calls=%fused_computation.2 | loop fusion | bytes 1310720 | tf_op jit(solution)/shard_map/broadcast_in_dim | solution.py:827
  132.5 0.6 pad_maximum_fusion.2
Async XLA Ops:
  0.6 5.0 %copy-start.5 = (f32[4,320,128]{2,1,0:T(8,128)S(1)}, f32[4,320,128]{2,1,0:T(8,128)}, u32[]{:S(2)}) copy-start(f32[4,320,128]{2,1,0:T(8,128)} %constant.19.clone.g_ref) | copy-start | bytes 1966084
  4.3 15.1 %copy-start.6 = (f32[16,1,4,320]{3,0,2,1:T(8,128)}, f32[16,1,4,320]{3,0,2,1:T(8,128)S(1)}, u32[]{:S(2)}) copy-start(f32[16,1,4,320]{3,0,2,1:T(8,128)S(1)} %copy.33) | copy-start | bytes 245764
  5.6 22.4 %copy-start = (bf16[4,2,8,16,320]{4,3,2,1,0:T(8,128)(2,1)}, bf16[4,2,8,16,320]{4,3,2,1,0:T(8,128)(2,1)S(1)}, u32[]{:S(2)}) copy-start(bf16[4,2,8,16,320]{4,3,2,1,0:T(8,128)(2,1)S(1)} %copy.22) | copy-start | bytes 1966084
  15.1 0.9 copy-start.3
  16.0 0.9 copy-start.4
  16.9 0.6 copy-start.10
  17.6 0.6 copy-start.11
  28.0 12.1 %copy-start.1 = (bf16[4,2,8,16,320]{4,3,2,1,0:T(8,128)(2,1)S(1)}, bf16[4,2,8,16,320]{4,3,2,1,0:T(8,128)(2,1)}, u32[]{:S(2)}) copy-start(bf16[4,2,8,16,320]{4,3,2,1,0:T(8,128)(2,1)} %copy-done) | copy-start | bytes 1966084
  28.0 12.1 %copy-start.7 = (f32[16,1,4,320]{3,0,2,1:T(8,128)S(1)}, f32[16,1,4,320]{3,0,2,1:T(8,128)}, u32[]{:S(2)}) copy-start(f32[16,1,4,320]{3,0,2,1:T(8,128)} %copy-done.6) | copy-start | bytes 245764
  40.1 1.0 copy-start.2
  78.7 0.7 copy-start.8
  79.4 0.8 copy-start.9
  80.2 0.6 copy-start.12
  80.8 0.9 copy-start.13
  81.6 12.6 %copy-start.15 = (bf16[4,16,320]{2,1,0:T(8,128)(2,1)S(1)}, bf16[4,16,320]{2,1,0:T(8,128)(2,1)}, u32[]{:S(2)}) copy-start(bf16[4,16,320]{2,1,0:T(8,128)(2,1)} %get-tuple-element.31) | copy-start | bytes 122884
  93.7 13.6 %collective-permute-start = (bf16[4,128,320]{2,1,0:T(8,128)(2,1)}, bf16[4,128,320]{2,1,0:T(8,128)(2,1)S(1)}, u32[]{:S(2)}, u32[]{:S(2)}) collective-permute-start(bf16[4,128,320]{2,1,0:T(8,128)(2,1)} %shard_map.194), channel_id=1, source_target_pairs={{0,1},{1,0},{2,3},{3,2},{4,5},{5,4},{6,7},{7,6},{8,9},{9,8},{10,11... | collective-permute-start | bytes 983048 | tf_op jit(solution)/shard_map/ppermute | solution.py:785
  94.8 12.5 %copy-start.14 = (bf16[4,128,320]{2,1,0:T(8,128)(2,1)S(1)}, bf16[4,128,320]{2,1,0:T(8,128)(2,1)}, u32[]{:S(2)}) copy-start(bf16[4,128,320]{2,1,0:T(8,128)(2,1)} %shard_map.194) | copy-start | bytes 983044

commit v3 on v2

--- a/solution.py
+++ b/solution.py
@@ -196,7 +196,8 @@
     mine[8:] = image_sums(frames, 2, x_ref, t_ref, g_ref)
     slots[tile] = mine[...]
     pl.semaphore_wait(pltpu.get_barrier_semaphore(), tiles - 1)
-    halo = Halo(tile, tiles, (x_ref, t_ref), (x_lo, t_lo), (x_hi, t_hi), halo_send, halo_recv)
+    sketches = t_ref.at[:, : t_ref.shape[1] // 2]
+    halo = Halo(tile, tiles, (x_ref, sketches), (x_lo, t_lo), (x_hi, t_hi), halo_send, halo_recv)
     sends = tile_sends(tile, tiles, mine, slots, send_sem, recv_sem)
     for copy in sends:
         copy.start()
@@ -715,16 +716,21 @@
             ),
         )(*args)
 
+    half = jax.ShapeDtypeStruct((cols, padded * frames, C), BF16)
     sums, x_lo, x_hi, p_lo, p_hi = exchange(
         functools.partial(input_kernel, frames),
         (x, p, group),
-        [like(x), like(x), like(p), like(p)],
+        [like(x), like(x), half, half],
         [anywhere] * 4,
         8 + padded,
         2,
         0,
     )
     latent_sums, probe_sums = sums[:8], sums[8:]
+    tests, _ = lax.optimization_barrier((p[:, padded * frames :], sums))
+    forward = [(i, i + 1) for i in range(tiles - 1)]
+    test_lo = lax.ppermute(tests, "tile", forward)
+    test_hi = lax.ppermute(tests, "tile", [(j, i) for i, j in forward])
     wqkv = jnp.swapaxes(w_qkv, 0, 1)
     primal = pl.pallas_call(
         functools.partial(primal_kernel, members),
@@ -763,6 +769,7 @@
     def tangent(lo, mid, hi, offset, sums, which, dtype):
         fixed = (latent_sums, w_spatial, w_temporal, wqkv, w_out, group_t, hh, hrow) + tuple(caches)
         moving = pl.BlockSpec((cols, per, C), lambda i: (0, i + offset, 0))
+        side = pl.BlockSpec((cols, per, C), lambda i: (0, i, 0))
         stat = pl.BlockSpec((CHUNK, 128), lambda i: (i, 0))
         return call(
             functools.partial(tangent_kernel, members, which),
@@ -773,7 +780,7 @@
             sums,
             *fixed,
             grid=(chunks,),
-            in_specs=[moving] * 3 + [stat] + [vmem] * len(fixed),
+            in_specs=[side, moving, side, stat] + [vmem] * len(fixed),
             out_specs=pl.BlockSpec((cols, per, C), lambda i: (0, i, 0)),
             flops=2 * 10**9,
         )
@@ -796,7 +803,7 @@
         1,
         [(shares - 1,), (shares - 1,)],
     )
-    test = tangent(p_lo, p, p_hi, chunks, probe_sums, 1, F32)
+    test = tangent(test_lo, p, test_hi, chunks, probe_sums, 1, F32)
     second = tangent(s_lo, sketch, s_hi, 0, gram, 0, BF16)
     js_all = from_shares(second[:, : own * frames])
     image = (cols, padded * frames, C)

time: 135 us -> 139 us (1.030)
  Pallas kernels: 108 us -> 100 us
  waiting for transfers between devices: 0.01 us -> 5.56 us
  starting transfers between devices: 0.51 us -> 5.08 us
    pallas_call x2, Pallas kernels: 47 us -> 38.6 us  [exchange(): pl.pallas_call(kernel, in_specs=[vmem] * len(args), out_shape=[jax.ShapeD...]
    ppermute x1, waiting for transfers between devices: 0.01 us -> 5.56 us  [from_shares(): blocks.append(lax.ppermute(block, 'probe', ring))]
    ppermute x0 -> x2, starting transfers between devices: none -> 4.57 us  [the longest x1 3.28 us: on_device(): test_lo = lax.ppermute(tests, 'tile', forward)]
    unnamed x34 -> x36, local copies, waits for them, and re-layouts: 8.57 us -> 9.83 us
  transfers between devices with their start and end apart: 1 -> 3, of which waited for: 0 -> 1; matrix products, arithmetic and copies ran while one was open for 0% -> 2% of each run, Pallas kernels for 9% -> 0%
where the time goes in v3:
time: 139 us
  Pallas kernels  100 us (72%)
  local copies, waits for them, and re-layouts  20.6 us (15%)
  waiting for transfers between devices  5.56 us (4%)
  starting transfers between devices  5.08 us (4%)
  other arithmetic  3.83 us (3%)
  between operations  3.23 us (2%)
    pallas_call x2, Pallas kernels, exchange(): pl.pallas_call(kernel, in_specs=[vmem] * len(args), out_shape=[jax.ShapeD...  38.6 us
    pallas_call x3, Pallas kernels, call(): pl.pallas_call(kernel, out_shape=out_shape, compiler_params=pltpu.Compile...  36.3 us
    pallas_call x1, Pallas kernels, reduce_over(): pl.pallas_call(functools.partial(reduce_kernel, axes), out_shape=jax.Shap...  10.1 us
    unnamed x36, local copies, waits for them, and re-layouts  9.83 us
    pallas_call x1, Pallas kernels, on_device(): pl.pallas_call(functools.partial(primal_kernel, members), in_specs=[smem]...  8.58 us
    pallas_call x1, Pallas kernels, on_device(): pl.pallas_call(functools.partial(combine_kernel, frames, ns, own, total),...  6.63 us
    ppermute x1, waiting for transfers between devices, from_shares(): blocks.append(lax.ppermute(block, 'probe', ring))  5.56 us
    ppermute x1, starting transfers between devices, on_device(): test_lo = lax.ppermute(tests, 'tile', forward)  3.28 us
  transfers between devices with their start and end apart: 3, of which 1 were waited for; matrix products, arithmetic and copies ran while one was open for 2% of the time, Pallas kernels for 0%

profile of v3, /device:TPU:0, one launch (start us, length us, event | category | flops | bytes accessed | tf_op | source)
XLA Modules:
  0.0 138.5 jit_solution(9862216714221738908)
XLA Ops:
  0.6 0.0 copy-start.3
  0.6 0.7 stack.29
  1.4 0.7 stack.30
  2.1 0.7 stack.31
  2.8 0.7 stack.32
  3.4 0.9 copy.33
  4.3 0.0 copy-start.4
  4.3 1.3 copy.22
  5.6 0.0 copy-start
  5.6 0.0 copy-done.3
  5.6 9.5 %shard_map.190 = (f32[16,128]{1,0:T(8,128)S(1)}, f32[4,16,320]{2,1,0:T(8,128)S(1)}, f32[4,16,320]{2,1,0:T(8,128)S(1)}, bf16[4,128,320]{2,1,0:T(8,128)(2,1)S(1)}, bf16[4,128,320]{2,1,0:T(8,128)(2,1)S(1)}) custom-call(f32[4,16,320]{2,1,0:T(8,128)S(1)} %bitcast.41, bf16[4,256,320]{2,1,0:T(8,128)(2,1)S(1)} %bitcast.35, f32[4,320,128]{2,1,0:T(8,128)S(1)} %copy-done.3), custom_call_target="tpu_custom_call" | custom-call | tf_op jit(solution)/shard_map/pallas_call | solution.py:698
  15.1 0.0 copy-start.6
  15.1 0.7 copy-done.6
  15.9 0.0 copy-start.7
  15.9 0.8 copy-done.7
  16.7 0.0 copy-start.10
  16.7 0.6 copy-done.10
  17.3 0.0 copy-start.11
  17.3 0.6 copy-done.11
  17.9 0.6 fusion.1
  18.5 0.6 pad_maximum_fusion.1.vec_ref
  19.1 0.0 copy-done.4
  19.1 8.6 %shard_map.191 = (bf16[4,16,320]{2,1,0:T(8,128)(2,1)}, f32[3,4,16,320]{3,2,1,0:T(8,128)}, f32[3,4,16,320]{3,2,1,0:T(8,128)}, f32[6,4,16,320]{3,2,1,0:T(8,128)}, ...) custom-call(f32[8]{0:T(128)} %temper_ref.1, ...), custom_call_target="tpu_custom_call" | custom-call | flops 100000000 | bytes 10000000 | tf_op jit(solution)/shard_map/pallas_call | solution.py:735
  27.7 0.0 copy-done
  27.7 0.0 copy-start.1
  27.7 0.0 copy-start.5
  27.7 12.1 %shard_map.192.s_ref.t_ref = bf16[4,128,320]{2,1,0:T(8,128)(2,1)} custom-call(bf16[4,128,320]{2,1,0:T(8,128)(2,1)} %copy-done.6, bf16[4,256,320]{2,1,0:T(8,128)(2,1)} %bitcast.36, bf16[4,128,320]{2,1,0:T(8,128)(2,1)} %copy-done.7, f32[8,128]{1,0:T(8,128)} %get-tuple-element.62.sums_ref, f32[8,128]{1,0:T(8,128)} %get-tuple-element.63.ls_ref, ...), custom_call_target="tpu_custom_call" | custom-call | flops 2000000000 | bytes 8718336 | tf_op jit(solution)/shard_map/pallas_call | solution.py:66
  39.8 0.0 copy-done.1
  39.8 0.0 copy-done.5
  39.9 0.0 copy-start.2
  39.9 1.0 copy-done.2
  40.8 29.1 %shard_map.193 = (f32[8,128]{1,0:T(8,128)S(1)}, bf16[2,4,128,320]{3,2,1,0:T(8,128)(2,1)S(1)}, bf16[4,128,320]{2,1,0:T(8,128)(2,1)S(1)}, bf16[4,128,320]{2,1,0:T(8,128)(2,1)S(1)}) custom-call(f32[4,16,320]{2,1,0:T(8,128)S(1)} %bitcast.43, bf16[4,128,320]{2,1,0:T(8,128)(2,1)S(1)} %copy-done.2, bf16[4,256,320]{2,1,0:T(8,128)(2,1)S(1)} %bitcast.39, ...), custom_call_target="tpu_custom_call" | custom-call | tf_op jit(solution)/shard_map/pallas_call | solution.py:698
  70.0 0.0 copy-start.8
  70.0 0.7 copy-done.8
  70.7 0.0 copy-start.9
  70.7 0.8 copy-done.9
  71.5 0.0 copy-start.12
  71.5 0.6 copy-done.12
  72.1 0.0 copy-start.13
  72.1 0.9 copy-done.13
  73.0 0.0 copy-start.16
  73.0 12.0 %shard_map.194 = bf16[4,128,320]{2,1,0:T(8,128)(2,1)} custom-call(bf16[4,128,320]{2,1,0:T(8,128)(2,1)} %copy-done.8, bf16[4,128,320]{2,1,0:T(8,128)(2,1)} %shard_map.192.s_ref.t_ref, bf16[4,128,320]{2,1,0:T(8,128)(2,1)} %copy-done.9, f32[8,128]{1,0:T(8,128)} %copy-done.12, f32[8,128]{1,0:T(8,128)} %get-tuple-element.63.ls_ref, bf16[9,320,320]{2,1,0:T(8,128)(2,1)} %ws_ref.7, ...), custom_call_target="tpu_custom_call" | custom-call | flops 2000000000 | bytes 8390656 | tf_op jit(solution)/shard_map/pallas_call | solution.py:66
  85.1 0.5 collective-permute-start
  85.6 1.3 collective-permute-start.2
  86.9 3.3 %collective-permute-start.1 = (bf16[4,128,320]{2,1,0:T(8,128)(2,1)S(1)}, bf16[4,128,320]{2,1,0:T(8,128)(2,1)S(1)}, u32[]{:S(2)}, u32[]{:S(2)}) collective-permute-start(bf16[4,128,320]{2,1,0:T(8,128)(2,1)S(1)} %slice.33), channel_id=1, source_target_pairs={{0,2},{2,4},{4,6},{6,8},{8,10},{10,12},{12,14},{14,16},{16,18},{18... | collective-permute-start | bytes 983048 | tf_op jit(solution)/shard_map/ppermute | solution.py:732
  90.2 0.0 copy-done.16
  90.2 0.6 copy.27
  90.8 5.6 %collective-permute-done = bf16[4,128,320]{2,1,0:T(8,128)(2,1)S(1)} collective-permute-done((bf16[4,128,320]{2,1,0:T(8,128)(2,1)}, bf16[4,128,320]{2,1,0:T(8,128)(2,1)S(1)}, u32[]{:S(2)}, u32[]{:S(2)}) %collective-permute-start) | collective-permute-done | bytes 327712 | tf_op jit(solution)/shard_map/ppermute | solution.py:792
  96.4 2.1 %pad_maximum_fusion.js_ref = bf16[2,4,128,320]{3,2,1,0:T(8,128)(2,1)} fusion(bf16[1,4,128,320]{3,2,1,0:T(8,128)(2,1)S(1)} %bitcast.54, bf16[1,4,128,320]{3,2,1,0:T(8,128)(2,1)} %bitcast.48), kind=kLoop, calls=%fused_computation | loop fusion | flops 327680 | bytes 1310720 | tf_op jit(solution)/shard_map/stack | solution.py:793
  98.5 0.0 collective-permute-done.2.hi_ref
  98.5 0.0 copy-start.14
  98.5 0.0 collective-permute-done.1.lo_ref
  98.5 0.7 copy-done.14
  99.2 0.7 copy-done.15
  100.0 12.2 %shard_map.195.jt_ref = f32[4,128,320]{2,1,0:T(8,128)} custom-call(bf16[4,128,320]{2,1,0:T(8,128)(2,1)} %copy-done.15, bf16[4,256,320]{2,1,0:T(8,128)(2,1)} %bitcast.37, bf16[4,128,320]{2,1,0:T(8,128)(2,1)} %copy-done.14, f32[8,128]{1,0:T(8,128)} %get-tuple-element.62.sums_ref, f32[8,128]{1,0:T(8,128)} %get-tuple-element.63.ls_ref, ...), custom_call_target="tpu_custom_call" | custom-call | flops 2000000000 | bytes 8718336 | tf_op jit(solution)/shard_map/pallas_call | solution.py:66
  112.1 6.6 %shard_map.196 = (f32[4,128,320]{2,1,0:T(8,128)}, bf16[4,128,320]{2,1,0:T(8,128)(2,1)}, bf16[4,128,320]{2,1,0:T(8,128)(2,1)}, f32[8,128]{1,0:T(8,128)}) custom-call(f32[8,128]{1,0:T(8,128)} %copy-done.12, bf16[2,4,128,320]{3,2,1,0:T(8,128)(2,1)} %copy-done.13, bf16[2,4,128,320]{3,2,1,0:T(8,128)(2,1)} %pad_maximum_fusion.js_ref, ...), custom_call_target="tpu_custom_call" | custom-call | flops 1000000000 | bytes 10000000 | tf_op jit(solution)/shard_map/pallas_call | solution.py:810
  118.8 2.5 %copy.32 = f32[4,8,16,320]{3,0,2,1:T(4,128)} copy(f32[4,8,16,320]{3,2,1,0:T(8,128)} %bitcast.51) | data formatting | bytes 1310720 | tf_op jit(solution)/shard_map/reshape | solution.py:833
  121.3 10.1 %shard_map.197 = f32[8,128]{1,0:T(8,128)} custom-call(f32[8,128]{1,0:T(8,128)} %get-tuple-element.51.x_ref), custom_call_target="tpu_custom_call" | custom-call | tf_op jit(solution)/shard_map/pallas_call | solution.py:313
  131.4 0.7 copy.26
  132.2 0.6 slice_reduce_fusion
  134.1 0.1 div.30
  134.2 0.1 div.28
  134.2 2.6 %copy_bitcast_fusion.1 = (bf16[8,16,1,4,320]{4,3,2,1,0:T(4,128)(2,1)}, bf16[8,16,1,4,320]{4,3,2,1,0:T(4,128)(2,1)}) fusion(bf16[4,8,16,320]{3,2,1,0:T(8,128)(2,1)} %bitcast.53, bf16[4,8,16,320]{3,2,1,0:T(8,128)(2,1)} %bitcast.52), kind=kLoop, calls=%fused_computation.2 | loop fusion | bytes 1310720 | tf_op jit(solution)/shard_map/broadcast_in_dim | solution.py:834
  136.8 0.6 pad_maximum_fusion.2
  (2 shorter events, 0.0 us)
Async XLA Ops:
  0.6 5.0 %copy-start.3 = (f32[4,320,128]{2,1,0:T(8,128)S(1)}, f32[4,320,128]{2,1,0:T(8,128)}, u32[]{:S(2)}) copy-start(f32[4,320,128]{2,1,0:T(8,128)} %constant.19.clone.g_ref) | copy-start | bytes 1966084
  4.3 14.8 %copy-start.4 = (f32[16,1,4,320]{3,0,2,1:T(8,128)}, f32[16,1,4,320]{3,0,2,1:T(8,128)S(1)}, u32[]{:S(2)}) copy-start(f32[16,1,4,320]{3,0,2,1:T(8,128)S(1)} %copy.33) | copy-start | bytes 245764
  5.6 22.1 %copy-start = (bf16[4,2,8,16,320]{4,3,2,1,0:T(8,128)(2,1)}, bf16[4,2,8,16,320]{4,3,2,1,0:T(8,128)(2,1)S(1)}, u32[]{:S(2)}) copy-start(bf16[4,2,8,16,320]{4,3,2,1,0:T(8,128)(2,1)S(1)} %copy.22) | copy-start | bytes 1966084
  15.1 0.8 copy-start.6
  15.9 0.8 copy-start.7
  16.7 0.6 copy-start.10
  17.3 0.6 copy-start.11
  27.7 12.1 %copy-start.1 = (bf16[4,2,8,16,320]{4,3,2,1,0:T(8,128)(2,1)S(1)}, bf16[4,2,8,16,320]{4,3,2,1,0:T(8,128)(2,1)}, u32[]{:S(2)}) copy-start(bf16[4,2,8,16,320]{4,3,2,1,0:T(8,128)(2,1)} %copy-done) | copy-start | bytes 1966084
  27.7 12.1 %copy-start.5 = (f32[16,1,4,320]{3,0,2,1:T(8,128)S(1)}, f32[16,1,4,320]{3,0,2,1:T(8,128)}, u32[]{:S(2)}) copy-start(f32[16,1,4,320]{3,0,2,1:T(8,128)} %copy-done.4) | copy-start | bytes 245764
  39.9 1.0 copy-start.2
  70.0 0.7 copy-start.8
  70.7 0.8 copy-start.9
  71.5 0.6 copy-start.12
  72.1 0.9 copy-start.13
  73.0 17.2 %copy-start.16 = (bf16[4,16,320]{2,1,0:T(8,128)(2,1)S(1)}, bf16[4,16,320]{2,1,0:T(8,128)(2,1)}, u32[]{:S(2)}) copy-start(bf16[4,16,320]{2,1,0:T(8,128)(2,1)} %get-tuple-element.32) | copy-start | bytes 122884
  85.1 11.3 %collective-permute-start = (bf16[4,128,320]{2,1,0:T(8,128)(2,1)}, bf16[4,128,320]{2,1,0:T(8,128)(2,1)S(1)}, u32[]{:S(2)}, u32[]{:S(2)}) collective-permute-start(bf16[4,128,320]{2,1,0:T(8,128)(2,1)} %shard_map.194), channel_id=1, source_target_pairs={{0,1},{1,0},{2,3},{3,2},{4,5},{5,4},{6,7},{7,6},{8,9},{9,8},{10,11... | collective-permute-start | bytes 983048 | tf_op jit(solution)/shard_map/ppermute | solution.py:792
  85.6 12.9 %collective-permute-start.2 = (bf16[4,128,320]{2,1,0:T(8,128)(2,1)S(1)}, bf16[4,128,320]{2,1,0:T(8,128)(2,1)S(1)}, u32[]{:S(2)}, u32[]{:S(2)}) collective-permute-start(bf16[4,128,320]{2,1,0:T(8,128)(2,1)S(1)} %slice.33), channel_id=1, source_target_pairs={{2,0},{4,2},{6,4},{8,6},{10,8},{12,10},{14,12},{16,14},{18,16},{20... | collective-permute-start | bytes 983048 | tf_op jit(solution)/shard_map/ppermute | solution.py:733
  86.9 11.6 %collective-permute-start.1 = (bf16[4,128,320]{2,1,0:T(8,128)(2,1)S(1)}, bf16[4,128,320]{2,1,0:T(8,128)(2,1)S(1)}, u32[]{:S(2)}, u32[]{:S(2)}) collective-permute-start(bf16[4,128,320]{2,1,0:T(8,128)(2,1)S(1)} %slice.33), channel_id=1, source_target_pairs={{0,2},{2,4},{4,6},{6,8},{8,10},{10,12},{12,14},{14,16},{16,18},{18... | collective-permute-start | bytes 983048 | tf_op jit(solution)/shard_map/ppermute | solution.py:732
  98.5 0.7 copy-start.14
  99.2 0.7 copy-start.15
